TPU v7x, 32 devices: a whole 2x2x4 slice. The times are simulated.
32 devices in a mesh: wide: 8 (over z, y), narrow: 4 (over x, core).
Axes of the slice: x: 2, y: 2, z: 4, core: 2. Of those that a mesh axis runs over, the one named last changes fastest.
Arguments:
- panel: float32 [16384, 128], P(('wide', 'narrow')), may hold values from -40 to 40
- trailing: float32 [16384, 256], P(('wide', 'narrow')), may hold values from -40 to 40
Outputs:
- q_factor: float32 [16384, 128], P(('wide', 'narrow'))
- r_factor: float32 [128, 128], replicated
- projection: float32 [128, 256], replicated
- updated: float32 [16384, 256], P(('wide', 'narrow'))
All inputs are finite; a program needn't handle non-finite values.
Results may differ from a plain program's by a relative error of at most 0.00045.
Values sent between devices are 32-bit elements; how exact they have to be, the bound alone decides.
No kernel may reach another device: no remote copies, remote signals or barrier semaphores. Data moves between devices by JAX's collectives and lax.ppermute only.
A program may use at most 64 MiB of HBM per device.

v0:
```python
import jax
import jax.numpy as jnp
from jax import lax
from jax.sharding import PartitionSpec as P


def upper_factor(gram_matrix):
    order = gram_matrix.shape[0]
    columns = jnp.arange(order, dtype=jnp.int32)

    def column_step(index, state):
        work, factor = state
        where = jnp.asarray(index).astype(jnp.int32)
        pivot_row = lax.dynamic_index_in_dim(work, where, 0, keepdims=False)
        pivot = lax.dynamic_index_in_dim(pivot_row, where, 0, keepdims=False)
        new_row = jnp.where(
            columns >= where, pivot_row / jnp.sqrt(pivot), jnp.zeros_like(pivot_row)
        )
        work = work - new_row[:, None] * new_row[None, :]
        factor = lax.dynamic_update_slice_in_dim(factor, new_row[None, :], where, 0)
        return (work, factor)

    start = (gram_matrix, jnp.zeros_like(gram_matrix))
    return lax.fori_loop(0, order, column_step, start)[1]


def inverse_upper(upper_part):
    order = upper_part.shape[0]
    identity = jnp.eye(order, dtype=upper_part.dtype)

    def row_step(count, inverse):
        where = (order - 1 - jnp.asarray(count)).astype(jnp.int32)
        upper_row = lax.dynamic_index_in_dim(upper_part, where, 0, keepdims=False)
        unit_row = lax.dynamic_index_in_dim(identity, where, 0, keepdims=False)
        pivot = lax.dynamic_index_in_dim(upper_row, where, 0, keepdims=False)
        partial_value = jnp.dot(upper_row, inverse, precision=lax.Precision.HIGHEST)
        new_row = (unit_row - partial_value) / pivot
        return lax.dynamic_update_slice_in_dim(inverse, new_row[None, :], where, 0)

    return lax.fori_loop(0, order, row_step, jnp.zeros_like(upper_part))


def product(left, right):
    return jnp.dot(left, right, precision=lax.Precision.HIGHEST, preferred_element_type=jnp.float32)


def on_device(panel, trailing):
    row_total = float(panel.shape[0] * lax.axis_size("wide") * lax.axis_size("narrow"))
    gram_local = product(panel.T, panel) / row_total
    cross_local = product(panel.T, trailing) / row_total
    gram_first, cross_terms = lax.psum((gram_local, cross_local), ("wide", "narrow"))
    first_factor = upper_factor(gram_first)
    basis_rows = product(panel, inverse_upper(first_factor))
    gram_second = lax.psum(product(basis_rows.T, basis_rows) / row_total, ("wide", "narrow"))
    second_factor = upper_factor(gram_second)
    q_factor = product(basis_rows, inverse_upper(second_factor))
    r_factor = product(second_factor, first_factor)
    projection = product(inverse_upper(r_factor).T, cross_terms)
    updated = trailing - product(q_factor, projection)
    return (q_factor, r_factor, projection, updated)


def solution(mesh):
    in_specs = (P(("wide", "narrow"), None), P(("wide", "narrow"), None))
    out_specs = (P(("wide", "narrow"), None), P(), P(), P(("wide", "narrow"), None))
    return jax.shard_map(
        on_device, mesh=mesh, in_specs=in_specs, out_specs=out_specs, check_vma=False
    )
```

profile of v0, /device:TPU:0, one launch (start us, length us, event | category | flops | bytes accessed | tf_op | source)
XLA Modules:
  0.0 1208.3 jit_solution(7260193359423582820)
XLA Ops:
  7.2 0.9 copy-done
  8.1 1.2 convolution_multiply_fusion.2
  9.4 1.3 convolution_multiply_fusion
  10.7 125.6 %all-reduce.4.cloned.1.call-done = f32[128,128]{1,0:T(8,128)} async-done(((f32[128,128]{1,0:T(8,128)}), f32[128,128]{1,0:T(8,128)}) %all-reduce.4.cloned.1.call-update) | async-done | bytes 65552 | tf_op jit(solution)/shard_map/psum | solution.py:51
  136.3 0.8 copy-done.3
  137.1 188.3 %while.89 = (s32[]{:T(128)}, f32[128,128]{1,0:T(8,128)S(1)}, f32[128,128]{1,0:T(8,128)S(1)}, s32[]{:T(128)}, s32[]{:T(128)}, /*index=5*/s32[]{:T(128)}) while((s32[]{:T(128)}, f32[128,128]{1,0:T(8,128)S(1)}, f32[128,128]{1,0:T(8,128)S(1)}, s32[]{:T(128)}, s32[]{:T(128)}, /*index=5*/s32[]{:T(128)}) %tuple.212), condition=%wide.region_2.3_spmd.clone, body=%wide.region_1.0_spmd.clone.sunk | while | flops 33667 | bytes 138357 | solution.py:24
  325.4 185.2 %while.86 = (s32[]{:T(128)}, f32[128,128]{1,0:T(8,128)S(1)}, f32[128,128]{1,0:T(8,128)S(1)}, f32[128,128]{1,0:T(8,128)S(1)}, s32[]{:T(128)}, /*index=5*/s32[]{:T(128)}, s32[]{:T(128)}, s32[]{:T(128)}) while((s32[]{:T(128)}, f32[128,128]{1,0:T(8,128)S(1)}, f32[128,128]{1,0:T(8,128)S(1)}, f32[128,128]{1,0:T(8,128)S(1)}, s32[]{:T(128)}, ...), condition=%wide.region_4.5_spmd, body=%wide.region_3.4_spmd.sunk | while | flops 196871 | bytes 69287 | solution.py:40
  327.5 0.8 fusion.61
  328.9 0.8 fusion.61
  330.4 0.8 fusion.61
  331.8 0.8 fusion.61
  341.9 0.8 fusion.61
  343.4 0.8 fusion.61
  344.8 0.8 fusion.61
  346.3 0.8 fusion.61
  355.0 0.8 fusion.61
  356.4 0.8 fusion.61
  357.9 0.8 fusion.61
  359.3 0.8 fusion.61
  369.4 0.8 fusion.61
  370.9 0.8 fusion.61
  372.3 0.8 fusion.61
  373.8 0.8 fusion.61
  382.5 0.8 fusion.61
  383.9 0.8 fusion.61
  385.3 0.8 fusion.61
  386.8 0.8 fusion.61
  396.9 0.8 fusion.61
  398.4 0.8 fusion.61
  399.8 0.8 fusion.61
  401.3 0.8 fusion.61
  409.9 0.8 fusion.61
  411.4 0.8 fusion.61
  412.8 0.8 fusion.61
  414.3 0.8 fusion.61
  424.4 0.8 fusion.61
  425.9 0.8 fusion.61
  427.3 0.8 fusion.61
  428.8 0.8 fusion.61
  437.4 0.8 fusion.61
  438.9 0.8 fusion.61
  511.1 1.0 convolution_multiply_fusion.1
  512.1 126.4 %all-reduce.6.cloned.1.call-done = (f32[128,128]{1,0:T(8,128)}, f32[128,256]{1,0:T(8,128)}) async-done(((f32[128,128]{1,0:T(8,128)}, f32[128,256]{1,0:T(8,128)}), (f32[128,128]{1,0:T(8,128)}, f32[128,256]{1,0:T(8,128)})) %all-reduce.6.cloned.1.call-update) | async-done | bytes 196624 | tf_op jit(solution)/shard_map/psum | solution.py:54
  638.5 0.8 copy-done.2
  639.3 188.3 %while.90 = (s32[]{:T(128)}, f32[128,128]{1,0:T(8,128)S(1)}, f32[128,128]{1,0:T(8,128)S(1)}, s32[]{:T(128)}, s32[]{:T(128)}, /*index=5*/s32[]{:T(128)}) while((s32[]{:T(128)}, f32[128,128]{1,0:T(8,128)S(1)}, f32[128,128]{1,0:T(8,128)S(1)}, s32[]{:T(128)}, s32[]{:T(128)}, /*index=5*/s32[]{:T(128)}) %tuple.211), condition=%wide.region_7.8_spmd.clone, body=%wide.region_6.7_spmd.clone.sunk | while | flops 33667 | bytes 138357 | solution.py:24
  827.8 185.2 %while.88 = (s32[]{:T(128)}, f32[128,128]{1,0:T(8,128)S(1)}, f32[128,128]{1,0:T(8,128)S(1)}, f32[128,128]{1,0:T(8,128)S(1)}, s32[]{:T(128)}, /*index=5*/s32[]{:T(128)}, s32[]{:T(128)}, s32[]{:T(128)}) while((s32[]{:T(128)}, f32[128,128]{1,0:T(8,128)S(1)}, f32[128,128]{1,0:T(8,128)S(1)}, f32[128,128]{1,0:T(8,128)S(1)}, s32[]{:T(128)}, ...), condition=%wide.region_11.12_spmd, body=%wide.region_10.11_spmd.sunk | while | flops 196871 | bytes 69287 | solution.py:40
  1013.7 185.2 %while.87 = (s32[]{:T(128)}, f32[128,128]{1,0:T(8,128)S(1)}, f32[128,128]{1,0:T(8,128)S(1)}, f32[128,128]{1,0:T(8,128)S(1)}, s32[]{:T(128)}, /*index=5*/s32[]{:T(128)}, s32[]{:T(128)}, s32[]{:T(128)}) while((s32[]{:T(128)}, f32[128,128]{1,0:T(8,128)S(1)}, f32[128,128]{1,0:T(8,128)S(1)}, f32[128,128]{1,0:T(8,128)S(1)}, s32[]{:T(128)}, ...), condition=%wide.region_9.10_spmd, body=%wide.region_8.9_spmd.sunk | while | flops 196871 | bytes 69287 | solution.py:40
  1200.1 1.4 convolution_subtract_fusion
  (2681 shorter events, 706.1 us)
Async XLA Ops:
  7.2 1.0 copy-start
  7.2 2.2 copy-start.1
  7.2 129.1 %all-reduce.4.cloned.1.call-start = ((), (), s32[]{:S(2)}) async-start(), calls=%async_computation | async-start | bytes 131072 | tf_op jit(solution)/shard_map/psum | solution.py:51
  9.4 629.1 %all-reduce.6.cloned.1.call-start = ((), (), s32[]{:S(2)}) async-start(), calls=%async_computation.1 | async-start | bytes 393216 | tf_op jit(solution)/shard_map/psum | solution.py:54
  136.3 0.8 copy-start.3
  638.5 0.8 copy-start.2
  1013.0 0.6 copy-start.7
  1198.8 0.9 copy-start.6
  1199.4 2.0 copy-start.4
  1200.1 1.4 copy-start.5
Sparse Core Ops, SparseCore 0:
  14.2 122.0 all-reduce.3
  512.2 126.2 all-reduce.5
where the time goes:
time: 1220 us; the launch traced here: 1210 us
  local copies, waits for them, and re-layouts  401 us (33%)
  matrix products  313 us (26%)
  waiting for transfers between devices  252 us (21%)
  loops' own time  202 us (17%)
  other arithmetic  26.6 us (2%)
  between operations  14.2 us (1%)
    dot_general x384, matrix products, row_step(): partial_value = jnp.dot(upper_row, inverse, precision=lax.Precision.HIGHEST)  306 us
    dynamic_slice x384, local copies, waits for them, and re-layouts, row_step(): pivot = lax.dynamic_index_in_dim(upper_row, where, 0, keepdims=False)  226 us
    another operation x2, loops' own time, upper_factor(): return lax.fori_loop(0, order, column_step, start)[1]  190 us
    dynamic_slice x256, local copies, waits for them, and re-layouts, column_step(): pivot = lax.dynamic_index_in_dim(pivot_row, where, 0, keepdims=False)  151 us
    psum x1, waiting for transfers between devices, on_device(): lax.psum(product(basis_rows.T, basis_rows) / row_total, ('wide', 'narrow'))  126 us
    psum x1, waiting for transfers between devices, on_device(): lax.psum((gram_local, cross_local), ('wide', 'narrow'))  126 us
  transfers between devices with their start and end apart: 2, of which 2 were waited for; matrix products, arithmetic and copies ran while one was open for 0% of the time, Pallas kernels for 0%

commit v1 on v0

v1 whole, which is shorter than its diff:
```python
import functools

import jax
import jax.numpy as jnp
from jax import lax
from jax.experimental import pallas as pl
from jax.experimental.pallas import tpu as pltpu
from jax.sharding import PartitionSpec as P

AXES = ("wide", "narrow")
SUBLANES = 8
GRAM_SLICES = 5
FACTOR_SLICES = 5
VMEM = pl.BlockSpec(memory_space=pltpu.VMEM)


def product(left, right, contract=(1, 0)):
    dims = (((contract[0],), (contract[1],)), ((), ()))
    return lax.dot_general(
        left, right, dims, precision=lax.Precision.HIGHEST, preferred_element_type=jnp.float32
    )


def exact_product(left, right, contract):
    dims = (((contract[0],), (contract[1],)), ((), ()))
    return lax.dot_general(left, right, dims, preferred_element_type=jnp.float32)


def two_sum(left, right):
    total = left + right
    shown = total - left
    return total, (left - (total - shown)) + (right - shown)


def fixed_point_slices(value, peak, first_bits, count):
    sigma = peak * float(2 ** (24 - first_bits))
    terms = []
    for _ in range(count):
        term = (value + sigma) - sigma
        value = value - term
        terms.append(term.astype(jnp.bfloat16))
        sigma = sigma * float(2.0 ** -(first_bits + 1))
    return terms


def gram_kernel(panel_ref, trailing_ref, out_ref):
    panel = panel_ref[...]
    peak = jnp.max(jnp.abs(panel), axis=0, keepdims=True)
    terms = fixed_point_slices(panel, peak, 7, GRAM_SLICES)
    dot = functools.partial(exact_product, contract=(0, 0))
    first = dot(terms[0], terms[0])
    second = dot(terms[0], terms[1])
    rest = dot(terms[0], terms[2])
    rest = rest + dot(terms[1], terms[2]) + dot(terms[0], terms[3])
    rest = rest + dot(terms[0], terms[4]) + dot(terms[1], terms[3])
    rest = rest + rest.T + dot(terms[1], terms[1]) + dot(terms[2], terms[2])
    second, second_low = two_sum(second, second.T)
    high, high_low = two_sum(first, second)
    high, low = two_sum(high, high_low + (second_low + rest))
    cross = product(panel, trailing_ref[...], (0, 0))
    groups = high.shape[0] // SUBLANES
    for group in range(groups):
        rows = slice(group * SUBLANES, (group + 1) * SUBLANES)
        out_ref[2 * group * SUBLANES : (2 * group + 1) * SUBLANES, :] = high[rows]
        out_ref[(2 * group + 1) * SUBLANES : (2 * group + 2) * SUBLANES, :] = low[rows]
    width = high.shape[1]
    for part in range(cross.shape[1] // width):
        base = (2 + part) * high.shape[0]
        out_ref[base : base + high.shape[0], :] = cross[:, part * width : (part + 1) * width]


def sum_kernel(is_gram_ref, parts_ref, out_ref):
    half = parts_ref.shape[1] // 2
    highs = [parts_ref[d, :half, :] for d in range(parts_ref.shape[0])]
    lows = [parts_ref[d, half:, :] for d in range(parts_ref.shape[0])]
    plain = lows
    while len(highs) > 1:
        pairs = [two_sum(highs[i], highs[i + 1]) for i in range(0, len(highs), 2)]
        plain = [plain[i] + plain[i + 1] for i in range(0, len(plain), 2)]
        lows = [lows[i] + lows[i + 1] for i in range(0, len(lows), 2)]
        lows = [low + pair[1] for low, pair in zip(lows, pairs)]
        highs = [pair[0] for pair in pairs]
    high, low = two_sum(highs[0], lows[0])
    gram = jnp.full(high.shape, is_gram_ref[0], jnp.int32) != 0
    first = jnp.where(gram, high, highs[0])
    second = jnp.where(gram, low, plain[0])
    for d in range(parts_ref.shape[0]):
        out_ref[d, :half, :] = first
        out_ref[d, half:, :] = second


def factor_and_inverse(tiles):
    count = len(tiles)
    shape = tiles[0].shape
    lane = lax.broadcasted_iota(jnp.int32, shape, 1)
    sub = lax.broadcasted_iota(jnp.int32, shape, 0)
    over_lanes = lambda v, c: jnp.broadcast_to(v[:, c : c + 1], shape)
    over_rows = lambda v, i: jnp.broadcast_to(v[i : i + 1, :], shape)
    tiles = list(tiles)
    upper, lower = [], []
    for t in range(count):
        base = t * SUBLANES
        current = tiles[t]
        columns = {
            s: [over_lanes(tiles[s], base + c) for c in range(SUBLANES)] for s in range(t, count)
        }
        inside = (lane >= base) & (lane < base + SUBLANES)
        for s in range(t + 1, count):
            tiles[s] = jnp.where(inside, 0.0, tiles[s])
        pivots = jnp.zeros(shape, jnp.float32)
        for i in range(SUBLANES):
            k = base + i
            pivot = over_rows(columns[t][i], i)
            inverse = 1.0 / pivot
            pivots = jnp.where(sub == i, pivot, pivots)
            row = jnp.where(lane == k, 1.0, over_rows(current, i))
            later = {c: over_rows(columns[t][c], i) for c in range(i + 1, SUBLANES)}
            below = jnp.where((lane > k) & (lane < base + SUBLANES), 0.0, row)
            for s in range(t, count):
                multiplier = columns[s][i] * inverse
                if s == t:
                    if i == SUBLANES - 1:
                        continue
                    multiplier = jnp.where(sub > i, multiplier, 0.0)
                    current = jnp.where((lane == k) & (sub > i), 0.0, current) - multiplier * row
                else:
                    tiles[s] = tiles[s] - multiplier * below
                for c in later:
                    columns[s][c] = columns[s][c] - multiplier * later[c]
        scale = lax.rsqrt(pivots)
        scaled = current * scale
        diagonal = sub + base
        upper.append(jnp.where(lane >= diagonal, scaled, 0.0))
        lower.append(jnp.where(lane < diagonal, scaled, jnp.where(lane == diagonal, scale, 0.0)))
    return jnp.concatenate(upper, 0), jnp.concatenate(lower, 0)


def row_blocks(matrix):
    return [matrix[i : i + SUBLANES] for i in range(0, matrix.shape[0], SUBLANES)]


def final_kernel(row_total, sums_ref, panel_ref, trailing_ref, q_ref, r_ref, p_ref, u_ref):
    order = panel_ref.shape[1]
    groups = order // SUBLANES
    inverse_rows = 1.0 / row_total
    pick = lambda j: sums_ref[j * SUBLANES : (j + 1) * SUBLANES, :] * inverse_rows
    high_tiles = [pick(2 * g) for g in range(groups)]
    high = jnp.concatenate(high_tiles, 0)
    low = jnp.concatenate([pick(2 * g + 1) for g in range(groups)], 0)
    first_factor, first_inverse_t = factor_and_inverse(high_tiles)

    peak = jnp.max(jnp.abs(first_factor), axis=0, keepdims=True)
    terms = fixed_point_slices(first_factor, peak, 8, FACTOR_SLICES)
    orders = []
    for size in range(1, FACTOR_SLICES + 1):
        left = jnp.concatenate(terms[:size], 0)
        right = jnp.concatenate(terms[:size][::-1], 0)
        orders.append(exact_product(left, right, (0, 0)))
    remainder, error = two_sum(high, -orders[0])
    remainder, error_next = two_sum(remainder, -orders[1])
    rest = low - orders[2]
    for term in orders[3:]:
        rest = rest - term
    remainder = remainder + ((error + error_next) + rest)
    near_one_t = product(first_inverse_t, first_factor, (1, 1))
    near_one = product(first_factor, first_inverse_t, (1, 1))
    carried = product(remainder, first_inverse_t, (1, 1))
    gram_second = product(
        jnp.concatenate([near_one_t, first_inverse_t], 1), jnp.concatenate([near_one, carried], 0)
    )
    second_factor, second_inverse_t = factor_and_inverse(row_blocks(gram_second))

    r_ref[...] = product(second_factor, first_factor)
    inverse_t = product(second_inverse_t, first_inverse_t)
    parts = (sums_ref.shape[0] - 2 * order) // order
    cross = jnp.concatenate(
        [sums_ref[(2 + j) * order : (3 + j) * order, :] * inverse_rows for j in range(parts)], 1
    )
    projection = product(inverse_t, cross)
    p_ref[...] = projection
    q_factor = product(panel_ref[...], inverse_t, (1, 1))
    q_ref[...] = q_factor
    u_ref[...] = trailing_ref[...] - product(q_factor, projection)


def call(body, outs, n_in, specs=None):
    return pl.pallas_call(
        body,
        out_shape=[jax.ShapeDtypeStruct(shape, jnp.float32) for shape in outs],
        in_specs=specs or [VMEM] * n_in,
        out_specs=[VMEM] * len(outs),
    )


def on_device(panel, trailing):
    rows, order = panel.shape
    width = trailing.shape[1]
    devices = lax.axis_size(AXES)
    row_total = float(rows * devices)
    total = 2 * order + order * width // order
    (local,) = call(gram_kernel, [(total, order)], 2)(panel, trailing)

    depth = total // (2 * devices)
    pieces = SUBLANES // depth
    slots = local.reshape(total // (2 * SUBLANES), 2, pieces, depth, order)
    slots = slots.transpose(0, 2, 1, 3, 4).reshape(devices, 2 * depth, order)
    parts = lax.all_to_all(slots, AXES, 0, 0)
    is_gram = (lax.axis_index(AXES) * 2 * depth < 2 * order).astype(jnp.int32).reshape(1)
    specs = [pl.BlockSpec(memory_space=pltpu.SMEM), VMEM]
    (summed,) = call(sum_kernel, [(devices, 2 * depth, order)], 2, specs)(is_gram, parts)
    sums = lax.all_to_all(summed, AXES, 0, 0)
    sums = sums.reshape(total // (2 * SUBLANES), pieces, 2, depth, order)
    sums = sums.transpose(0, 2, 1, 3, 4).reshape(total, order)

    outs = [(rows, order), (order, order), (order, width), (rows, width)]
    return tuple(call(functools.partial(final_kernel, row_total), outs, 3)(sums, panel, trailing))


def solution(mesh):
    in_specs = (P(AXES, None), P(AXES, None))
    out_specs = (P(AXES, None), P(), P(), P(AXES, None))
    return jax.shard_map(
        on_device, mesh=mesh, in_specs=in_specs, out_specs=out_specs, check_vma=False
    )
```

time: 1220 us -> 50.5 us (0.04)
  local copies, waits for them, and re-layouts: 401 us -> 0.7 us
  matrix products: 313 us -> 0 us
  waiting for transfers between devices: 252 us -> 10.6 us
  loops' own time: 202 us -> 0 us
  other arithmetic: 26.6 us -> 0 us
  Pallas kernels: 0 us -> 17.1 us
  blocking collectives: 0 us -> 13.9 us
  between operations: 14.2 us -> 0.65 us
    dynamic_slice x640 -> x0, local copies, waits for them, and re-layouts: 377 us -> none  [the longest x384 226 us: row_step(): pivot = lax.dynamic_index_in_dim(upper_row, where, 0, keepdims=False)]
    dot_general x392 -> x0, matrix products: 313 us -> none  [the longest x384 306 us: row_step(): partial_value = jnp.dot(upper_row, inverse, precision=lax.Precision.HIGHEST)]
    psum x2 -> x0, waiting for transfers between devices: 252 us -> none  [the longest x1 126 us: on_device(): lax.psum(product(basis_rows.T, basis_rows) / row_total, ('wide', 'narrow'))]
    another operation x5 -> x0, loops' own time: 202 us -> none  [the longest x2 190 us: upper_factor(): return lax.fori_loop(0, order, column_step, start)[1]]
    dynamic_update_slice x640 -> x0, local copies, waits for them, and re-layouts: 21.3 us -> none  [the longest x384 11.7 us: row_step(): return lax.dynamic_update_slice_in_dim(inverse, new_row[None, :], where, 0)]
    sub x256 -> x0, other arithmetic: 21 us -> none  [column_step(): work = work - new_row[:, None] * new_row[None, :]]
    pallas_call x0 -> x3, Pallas kernels: none -> 17.1 us  [the longest x1 12.7 us: on_device(): call(functools.partial(final_kernel, row_total), outs, 3)]
    all_to_all x0 -> x1, blocking collectives: none -> 13.9 us  [on_device(): sums = lax.all_to_all(summed, AXES, 0, 0)]
  transfers between devices with their start and end apart: 2 -> 1, of which waited for: 2 -> 1; matrix products, arithmetic and copies ran while one was open for 0% -> 0% of each run, Pallas kernels for 0% -> 0%
where the time goes in v1:
time: 50.5 us; the launch traced here: 50.2 us
  Pallas kernels  17.1 us (34%)
  blocking collectives  13.9 us (28%)
  waiting for transfers between devices  10.6 us (21%)
  starting transfers between devices  7.33 us (15%)
  local copies, waits for them, and re-layouts  0.7 us (1%)
  between operations  0.65 us (1%)
    all_to_all x1, blocking collectives, on_device(): sums = lax.all_to_all(summed, AXES, 0, 0)  13.9 us
    pallas_call x1, Pallas kernels, on_device(): call(functools.partial(final_kernel, row_total), outs, 3)  12.7 us
    all_to_all x1, waiting for transfers between devices, on_device(): parts = lax.all_to_all(slots, AXES, 0, 0)  10.6 us
    all_to_all x1, starting transfers between devices, on_device(): parts = lax.all_to_all(slots, AXES, 0, 0)  7.33 us
    pallas_call x1, Pallas kernels, on_device(): local, = call(gram_kernel, [(total, order)], 2)(panel, trailing)  2.63 us
    pallas_call x1, Pallas kernels, on_device(): call(sum_kernel, [(devices, 2 * depth, order)], 2, specs)(is_gram, parts)  1.71 us
  transfers between devices with their start and end apart: 1, of which 1 were waited for; matrix products, arithmetic and copies ran while one was open for 0% of the time, Pallas kernels for 0%

profile of v1, /device:TPU:0, one launch (start us, length us, event | category | flops | bytes accessed | tf_op | source)
XLA Modules:
  0.0 50.2 jit_solution(1139800563396185412)
XLA Ops:
  0.6 2.6 %shard_map.57 = f32[512,128]{1,0:T(8,128)} custom-call(f32[512,128]{1,0:T(8,128)} %panel_ref.3, f32[512,256]{1,0:T(8,128)} %trailing_ref.3), custom_call_target="tpu_custom_call" | custom-call | tf_op jit(solution)/shard_map/pallas_call | solution.py:201
  3.3 7.3 %all-to-all-start = ((f32[32,16,128]{2,1,0:T(8,128)}), f32[32,16,128]{2,1,0:T(8,128)S(1)}, u32[]{:S(2)}, u32[]{:S(2)}) async-start(f32[32,16,128]{2,1,0:T(8,128)} %bitcast.3), calls=%async_computation | async-start | bytes 524288 | tf_op jit(solution)/shard_map/all_to_all | solution.py:207
  10.6 10.6 %all-to-all-done.parts_ref = f32[32,16,128]{2,1,0:T(8,128)S(1)} async-done(((f32[32,16,128]{2,1,0:T(8,128)}), f32[32,16,128]{2,1,0:T(8,128)S(1)}, u32[]{:S(2)}, u32[]{:S(2)}) %all-to-all-start) | async-done | bytes 262176 | tf_op jit(solution)/shard_map/all_to_all | solution.py:207
  21.2 0.0 copy-start
  21.2 0.7 %copy-done = f32[32,16,128]{2,1,0:T(8,128)} copy-done((f32[32,16,128]{2,1,0:T(8,128)}, f32[32,16,128]{2,1,0:T(8,128)S(1)}, u32[]{:S(2)}) %copy-start) | copy-done | bytes 262168
  21.9 1.7 %shard_map.58 = f32[32,16,128]{2,1,0:T(8,128)} custom-call(s32[1]{0:T(128)} %bitcast.is_gram_ref, f32[32,16,128]{2,1,0:T(8,128)} %copy-done), custom_call_target="tpu_custom_call" | custom-call | tf_op jit(solution)/shard_map/pallas_call | solution.py:210
  23.6 13.9 %all_to_all.10 = f32[32,16,128]{2,1,0:T(8,128)} all-to-all(f32[32,16,128]{2,1,0:T(8,128)} %shard_map.58), channel_id=1, replica_groups=mesh['wide'=8,'narrow'=4] {'wide','narrow'}, dimensions={0} | all-to-all | bytes 524288 | tf_op jit(solution)/shard_map/all_to_all | solution.py:211
  37.4 12.7 %shard_map.59 = (f32[512,128]{1,0:T(8,128)}, f32[128,128]{1,0:T(8,128)}, f32[128,256]{1,0:T(8,128)}, f32[512,256]{1,0:T(8,128)}) custom-call(f32[512,128]{1,0:T(8,128)} %bitcast.4, f32[512,128]{1,0:T(8,128)} %panel_ref.3, f32[512,256]{1,0:T(8,128)} %trailing_ref.3), custom_call_target="tpu_custom_call" | custom-call | tf_op jit(solution)/shard_map/pallas_call | solution.py:216
Async XLA Ops:
  3.3 17.9 %all-to-all-start = ((f32[32,16,128]{2,1,0:T(8,128)}), f32[32,16,128]{2,1,0:T(8,128)S(1)}, u32[]{:S(2)}, u32[]{:S(2)}) async-start(f32[32,16,128]{2,1,0:T(8,128)} %bitcast.3), calls=%async_computation | async-start | bytes 524288 | tf_op jit(solution)/shard_map/all_to_all | solution.py:207
  21.2 0.7 %copy-start = (f32[32,16,128]{2,1,0:T(8,128)}, f32[32,16,128]{2,1,0:T(8,128)S(1)}, u32[]{:S(2)}) copy-start(f32[32,16,128]{2,1,0:T(8,128)S(1)} %all-to-all-done.parts_ref) | copy-start | bytes 786436

commit v2 on v1

--- a/solution.py
+++ b/solution.py
@@ -58,35 +58,49 @@
     high, high_low = two_sum(first, second)
     high, low = two_sum(high, high_low + (second_low + rest))
     cross = product(panel, trailing_ref[...], (0, 0))
-    groups = high.shape[0] // SUBLANES
-    for group in range(groups):
-        rows = slice(group * SUBLANES, (group + 1) * SUBLANES)
-        out_ref[2 * group * SUBLANES : (2 * group + 1) * SUBLANES, :] = high[rows]
-        out_ref[(2 * group + 1) * SUBLANES : (2 * group + 2) * SUBLANES, :] = low[rows]
-    width = high.shape[1]
-    for part in range(cross.shape[1] // width):
-        base = (2 + part) * high.shape[0]
-        out_ref[base : base + high.shape[0], :] = cross[:, part * width : (part + 1) * width]
-
-
-def sum_kernel(is_gram_ref, parts_ref, out_ref):
-    half = parts_ref.shape[1] // 2
-    highs = [parts_ref[d, :half, :] for d in range(parts_ref.shape[0])]
-    lows = [parts_ref[d, half:, :] for d in range(parts_ref.shape[0])]
-    plain = lows
-    while len(highs) > 1:
-        pairs = [two_sum(highs[i], highs[i + 1]) for i in range(0, len(highs), 2)]
-        plain = [plain[i] + plain[i + 1] for i in range(0, len(plain), 2)]
-        lows = [lows[i] + lows[i + 1] for i in range(0, len(lows), 2)]
-        lows = [low + pair[1] for low, pair in zip(lows, pairs)]
-        highs = [pair[0] for pair in pairs]
-    high, low = two_sum(highs[0], lows[0])
-    gram = jnp.full(high.shape, is_gram_ref[0], jnp.int32) != 0
-    first = jnp.where(gram, high, highs[0])
-    second = jnp.where(gram, low, plain[0])
-    for d in range(parts_ref.shape[0]):
-        out_ref[d, :half, :] = first
-        out_ref[d, half:, :] = second
+    high_half, high_rest = pack_symmetric(high)
+    low_half, low_rest = pack_symmetric(low)
+    half = high_half.shape[0] // 2
+    width = cross.shape[1] // 2
+    for core in range(2):
+        rows = slice(core * half, (core + 1) * half)
+        blocks = [high_half[rows], high_rest, low_half[rows], low_rest]
+        blocks.append(cross[:, core * width : (core + 1) * width])
+        at = 0
+        for block in blocks:
+            out_ref[core, at : at + block.shape[0], :] = block
+            at += block.shape[0]
+
+
+def grid_of(shape):
+    return (lax.broadcasted_iota(jnp.int32, shape, d) for d in range(2))
+
+
+def pack_symmetric(matrix):
+    order = matrix.shape[0]
+    half = order // 2
+    top = matrix[:half]
+    bottom = pltpu.roll(matrix[half:], half, 1)
+    row, lane = grid_of(top.shape)
+    rest = jnp.sum(jnp.where(row == lane, bottom, 0.0), axis=0, keepdims=True)
+    return jnp.where(lane < row, bottom, top), jnp.broadcast_to(rest, (SUBLANES, order))
+
+
+def unpack_symmetric(packed, rest):
+    half, order = packed.shape
+    turned = packed.T
+    left, right = packed[:, :half], packed[:, half:]
+    row, lane = grid_of(left.shape)
+    diagonal = jnp.broadcast_to(rest[:1, :half], left.shape)
+    top = jnp.concatenate([jnp.where(lane >= row, left, turned[:half]), right], 1)
+    lower = jnp.where(lane < row, left, jnp.where(lane == row, diagonal, turned[:half]))
+    return jnp.concatenate([top, jnp.concatenate([turned[half:], lower], 1)], 0)
+
+
+def add_terms(left, right, pair_rows):
+    high, error = two_sum(left[:pair_rows], right[:pair_rows])
+    low = (left[pair_rows : 2 * pair_rows] + right[pair_rows : 2 * pair_rows]) + error
+    return jnp.concatenate([high, low, left[2 * pair_rows :] + right[2 * pair_rows :]], 0)
 
 
 def factor_and_inverse(tiles):
@@ -139,14 +153,23 @@
     return [matrix[i : i + SUBLANES] for i in range(0, matrix.shape[0], SUBLANES)]
 
 
-def final_kernel(row_total, sums_ref, panel_ref, trailing_ref, q_ref, r_ref, p_ref, u_ref):
+def final_kernel(row_total, core_ref, own_ref, other_ref, panel_ref, trailing_ref, q_ref, r_ref, p_ref, u_ref):
     order = panel_ref.shape[1]
-    groups = order // SUBLANES
     inverse_rows = 1.0 / row_total
-    pick = lambda j: sums_ref[j * SUBLANES : (j + 1) * SUBLANES, :] * inverse_rows
-    high_tiles = [pick(2 * g) for g in range(groups)]
-    high = jnp.concatenate(high_tiles, 0)
-    low = jnp.concatenate([pick(2 * g + 1) for g in range(groups)], 0)
+    swapped = jnp.full(own_ref.shape, core_ref[0], jnp.int32) != 0
+    own = own_ref[...] * inverse_rows
+    other = other_ref[...] * inverse_rows
+    halves = [jnp.where(swapped, other, own), jnp.where(swapped, own, other)]
+    quarter = order // 4
+    pair_rows = quarter + SUBLANES
+    pick = lambda at: unpack_symmetric(
+        jnp.concatenate([half[at : at + quarter] for half in halves], 0),
+        halves[0][at + quarter : at + pair_rows],
+    )
+    high = pick(0)
+    low = pick(pair_rows)
+    cross = jnp.concatenate([half[2 * pair_rows :] for half in halves], 1)
+    high_tiles = row_blocks(high)
     first_factor, first_inverse_t = factor_and_inverse(high_tiles)
 
     peak = jnp.max(jnp.abs(first_factor), axis=0, keepdims=True)
@@ -172,10 +195,6 @@
 
     r_ref[...] = product(second_factor, first_factor)
     inverse_t = product(second_inverse_t, first_inverse_t)
-    parts = (sums_ref.shape[0] - 2 * order) // order
-    cross = jnp.concatenate(
-        [sums_ref[(2 + j) * order : (3 + j) * order, :] * inverse_rows for j in range(parts)], 1
-    )
     projection = product(inverse_t, cross)
     p_ref[...] = projection
     q_factor = product(panel_ref[...], inverse_t, (1, 1))
@@ -183,37 +202,49 @@
     u_ref[...] = trailing_ref[...] - product(q_factor, projection)
 
 
-def call(body, outs, n_in, specs=None):
+def call(body, outs, n_in, specs=None, near=False):
     return pl.pallas_call(
         body,
-        out_shape=[jax.ShapeDtypeStruct(shape, jnp.float32) for shape in outs],
+        out_shape=[(pltpu.VMEM if near else jax.ShapeDtypeStruct)(shape, jnp.float32) for shape in outs],
         in_specs=specs or [VMEM] * n_in,
         out_specs=[VMEM] * len(outs),
     )
+
+
+def all_sum(blocks, pair_rows):
+    devices = lax.axis_size(AXES)
+    bits = devices.bit_length() - 1
+    send = lambda value, mask: lax.ppermute(value, AXES, [(i, i ^ mask) for i in range(devices)])
+    add = functools.partial(add_terms, pair_rows=pair_rows)
+    odd = lax.axis_index(AXES) % 2
+    own = jnp.where(odd == 0, blocks[0], blocks[1])
+    value = add(own, send(jnp.where(odd == 0, blocks[1], blocks[0]), 1))
+    stages = [(bit,) for bit in range(3, bits)]
+    stages.insert(1, (1, 2))
+    for stage in stages:
+        first = 1 << stage[0]
+        if len(stage) == 1:
+            value = add(value, send(value, first))
+        else:
+            second = 1 << stage[1]
+            near, far, across = [send(value, mask) for mask in (first, second, first | second)]
+            value = add(add(value, near), add(far, across))
+    return value, send(value, 1), odd
 
 
 def on_device(panel, trailing):
     rows, order = panel.shape
     width = trailing.shape[1]
-    devices = lax.axis_size(AXES)
-    row_total = float(rows * devices)
-    total = 2 * order + order * width // order
-    (local,) = call(gram_kernel, [(total, order)], 2)(panel, trailing)
-
-    depth = total // (2 * devices)
-    pieces = SUBLANES // depth
-    slots = local.reshape(total // (2 * SUBLANES), 2, pieces, depth, order)
-    slots = slots.transpose(0, 2, 1, 3, 4).reshape(devices, 2 * depth, order)
-    parts = lax.all_to_all(slots, AXES, 0, 0)
-    is_gram = (lax.axis_index(AXES) * 2 * depth < 2 * order).astype(jnp.int32).reshape(1)
-    specs = [pl.BlockSpec(memory_space=pltpu.SMEM), VMEM]
-    (summed,) = call(sum_kernel, [(devices, 2 * depth, order)], 2, specs)(is_gram, parts)
-    sums = lax.all_to_all(summed, AXES, 0, 0)
-    sums = sums.reshape(total // (2 * SUBLANES), pieces, 2, depth, order)
-    sums = sums.transpose(0, 2, 1, 3, 4).reshape(total, order)
-
+    row_total = float(rows * lax.axis_size(AXES))
+    pair_rows = order // 4 + SUBLANES
+    (local,) = call(gram_kernel, [(2, 2 * pair_rows + order, order)], 2, near=True)(panel, trailing)
+    own, other, odd = all_sum(local, pair_rows)
     outs = [(rows, order), (order, order), (order, width), (rows, width)]
-    return tuple(call(functools.partial(final_kernel, row_total), outs, 3)(sums, panel, trailing))
+    specs = [pl.BlockSpec(memory_space=pltpu.SMEM)] + [VMEM] * 4
+    body = functools.partial(final_kernel, row_total)
+    own, other = [pltpu.with_memory_space_constraint(v, pltpu.VMEM) for v in (own, other)]
+    core = odd.astype(jnp.int32).reshape(1)
+    return tuple(call(body, outs, 5, specs)(core, own, other, panel, trailing))
 
 
 def solution(mesh):

time: 50.5 us -> 40.1 us (0.79)
  blocking collectives: 13.9 us -> 0 us
  waiting for transfers between devices: 10.6 us -> 14.5 us
  starting transfers between devices: 7.33 us -> 9.82 us
  Pallas kernels: 17.1 us -> 14.7 us
  local copies, waits for them, and re-layouts: 0.7 us -> 0 us
    ppermute x0 -> x7, waiting for transfers between devices: none -> 14.5 us  [all_sum(): lax.ppermute(value, AXES, [(i, i ^ mask) for i in range(devices)])]
    all_to_all x1 -> x0, blocking collectives: 13.9 us -> none  [on_device(): sums = lax.all_to_all(summed, AXES, 0, 0)]
    all_to_all x1 -> x0, waiting for transfers between devices: 10.6 us -> none  [on_device(): parts = lax.all_to_all(slots, AXES, 0, 0)]
    ppermute x0 -> x7, starting transfers between devices: none -> 9.82 us  [all_sum(): lax.ppermute(value, AXES, [(i, i ^ mask) for i in range(devices)])]
    all_to_all x1 -> x0, starting transfers between devices: 7.33 us -> none  [on_device(): parts = lax.all_to_all(slots, AXES, 0, 0)]
    pallas_call x3 -> x2, Pallas kernels: 17.1 us -> 14.7 us  [the longest x1 12.7 us: on_device(): return tuple(call(body, outs, 5, specs)(core, own, other, panel, trailing))]
    unnamed x2 -> x0, local copies, waits for them, and re-layouts: 0.7 us -> none
  transfers between devices with their start and end apart: 1 -> 7, of which waited for: 1 -> 7; matrix products, arithmetic and copies ran while one was open for 0% -> 0% of each run, Pallas kernels for 0% -> 0%
where the time goes in v2:
time: 40.1 us; the launch traced here: 39.9 us
  Pallas kernels  14.7 us (37%)
  waiting for transfers between devices  14.5 us (36%)
  starting transfers between devices  9.82 us (24%)
  between operations  0.74 us (2%)
    ppermute x7, waiting for transfers between devices, all_sum(): lax.ppermute(value, AXES, [(i, i ^ mask) for i in range(devices)])  14.5 us
    pallas_call x1, Pallas kernels, on_device(): return tuple(call(body, outs, 5, specs)(core, own, other, panel, trailing))  12.7 us
    ppermute x7, starting transfers between devices, all_sum(): lax.ppermute(value, AXES, [(i, i ^ mask) for i in range(devices)])  9.82 us
    pallas_call x1, Pallas kernels, on_device(): call(gram_kernel, [(2, 2 * pair_rows + order, order)], 2, near=True)  2 us
  transfers between devices with their start and end apart: 7, of which 7 were waited for; matrix products, arithmetic and copies ran while one was open for 0% of the time, Pallas kernels for 0%

profile of v2, /device:TPU:0, one launch (start us, length us, event | category | flops | bytes accessed | tf_op | source)
XLA Modules:
  0.0 39.9 jit_solution(6777954590538161098)
XLA Ops:
  0.6 2.0 %shard_map.57 = f32[2,208,128]{2,1,0:T(8,128)S(1)} custom-call(f32[512,128]{1,0:T(8,128)} %panel_ref.3, f32[512,256]{1,0:T(8,128)} %trailing_ref.3), custom_call_target="tpu_custom_call" | custom-call | tf_op jit(solution)/shard_map/pallas_call | solution.py:240
  2.7 0.6 %collective-permute-start = (f32[208,128]{1,0:T(8,128)S(1)}, f32[208,128]{1,0:T(8,128)S(1)}, u32[]{:S(2)}, u32[]{:S(2)}) collective-permute-start(f32[208,128]{1,0:T(8,128)S(1)} %get-tuple-element.11), channel_id=1, source_target_pairs={{0,1},{1,0},{2,3},{3,2},{4,5},{5,4},{6,7},{7,6},{8,9},{9,8},{10,11... | collective-permute-start | bytes 319496 | tf_op jit(solution)/shard_map/ppermute | solution.py:217
  3.2 1.0 %collective-permute-done = f32[208,128]{1,0:T(8,128)S(1)} collective-permute-done((f32[208,128]{1,0:T(8,128)S(1)}, f32[208,128]{1,0:T(8,128)S(1)}, u32[]{:S(2)}, u32[]{:S(2)}) %collective-permute-start) | collective-permute-done | bytes 106528 | tf_op jit(solution)/shard_map/ppermute | solution.py:217
  4.2 3.0 %collective-permute-start.1 = (f32[208,128]{1,0:T(8,128)S(1)}, f32[208,128]{1,0:T(8,128)S(1)}, u32[]{:S(2)}, u32[]{:S(2)}) collective-permute-start(f32[208,128]{1,0:T(8,128)S(1)} %pad_maximum_fusion), channel_id=1, source_target_pairs={{0,8},{1,9},{2,10},{3,11},{4,12},{5,13},{6,14},{7,15},{8,0},{9,1},... | collective-permute-start | bytes 319496 | tf_op jit(solution)/shard_map/ppermute | solution.py:217
  7.2 3.3 %collective-permute-done.1 = f32[208,128]{1,0:T(8,128)S(1)} collective-permute-done((f32[208,128]{1,0:T(8,128)S(1)}, f32[208,128]{1,0:T(8,128)S(1)}, u32[]{:S(2)}, u32[]{:S(2)}) %collective-permute-start.1) | collective-permute-done | bytes 106528 | tf_op jit(solution)/shard_map/ppermute | solution.py:217
  10.6 2.7 %collective-permute-start.4 = (f32[208,128]{1,0:T(8,128)S(1)}, f32[208,128]{1,0:T(8,128)S(1)}, u32[]{:S(2)}, u32[]{:S(2)}) collective-permute-start(f32[208,128]{1,0:T(8,128)S(1)} %pad_maximum_fusion.1), channel_id=1, source_target_pairs={{0,6},{1,7},{2,4},{3,5},{4,2},{5,3},{6,0},{7,1},{8,14},{9,15},{10,... | collective-permute-start | bytes 319496 | tf_op jit(solution)/shard_map/ppermute | solution.py:217
  13.2 0.5 %collective-permute-start.3 = (f32[208,128]{1,0:T(8,128)S(1)}, f32[208,128]{1,0:T(8,128)S(1)}, u32[]{:S(2)}, u32[]{:S(2)}) collective-permute-start(f32[208,128]{1,0:T(8,128)S(1)} %pad_maximum_fusion.1), channel_id=1, source_target_pairs={{0,4},{1,5},{2,6},{3,7},{4,0},{5,1},{6,2},{7,3},{8,12},{9,13},{10,... | collective-permute-start | bytes 319496 | tf_op jit(solution)/shard_map/ppermute | solution.py:217
  13.7 0.4 collective-permute-start.2
  14.1 2.3 %collective-permute-done.4 = f32[208,128]{1,0:T(8,128)S(1)} collective-permute-done((f32[208,128]{1,0:T(8,128)S(1)}, f32[208,128]{1,0:T(8,128)S(1)}, u32[]{:S(2)}, u32[]{:S(2)}) %collective-permute-start.4) | collective-permute-done | bytes 106528 | tf_op jit(solution)/shard_map/ppermute | solution.py:217
  16.4 1.8 %collective-permute-done.3 = f32[208,128]{1,0:T(8,128)S(1)} collective-permute-done((f32[208,128]{1,0:T(8,128)S(1)}, f32[208,128]{1,0:T(8,128)S(1)}, u32[]{:S(2)}, u32[]{:S(2)}) %collective-permute-start.3) | collective-permute-done | bytes 106528 | tf_op jit(solution)/shard_map/ppermute | solution.py:217
  18.3 0.2 collective-permute-done.2
  18.6 2.7 %collective-permute-start.5 = (f32[208,128]{1,0:T(8,128)S(1)}, f32[208,128]{1,0:T(8,128)S(1)}, u32[]{:S(2)}, u32[]{:S(2)}) collective-permute-start(f32[208,128]{1,0:T(8,128)S(1)} %pad_maximum_fusion.2), channel_id=1, source_target_pairs={{0,16},{1,17},{2,18},{3,19},{4,20},{5,21},{6,22},{7,23},{8,24},{9,... | collective-permute-start | bytes 319496 | tf_op jit(solution)/shard_map/ppermute | solution.py:217
  21.2 4.5 %collective-permute-done.5 = f32[208,128]{1,0:T(8,128)S(1)} collective-permute-done((f32[208,128]{1,0:T(8,128)S(1)}, f32[208,128]{1,0:T(8,128)S(1)}, u32[]{:S(2)}, u32[]{:S(2)}) %collective-permute-start.5) | collective-permute-done | bytes 106528 | tf_op jit(solution)/shard_map/ppermute | solution.py:217
  25.8 0.1 collective-permute-start.6
  25.9 1.3 %collective-permute-done.6.other_ref = f32[208,128]{1,0:T(8,128)S(1)} collective-permute-done((f32[208,128]{1,0:T(8,128)S(1)}, f32[208,128]{1,0:T(8,128)S(1)}, u32[]{:S(2)}, u32[]{:S(2)}) %collective-permute-start.6) | collective-permute-done | bytes 106528 | tf_op jit(solution)/shard_map/ppermute | solution.py:217
  27.2 12.7 %shard_map.58 = (f32[512,128]{1,0:T(8,128)}, f32[128,128]{1,0:T(8,128)}, f32[128,256]{1,0:T(8,128)}, f32[512,256]{1,0:T(8,128)}) custom-call(s32[1]{0:T(128)} %bitcast.core_ref, f32[208,128]{1,0:T(8,128)S(1)} %pad_maximum_fusion.3.own_ref, f32[208,128]{1,0:T(8,128)S(1)} %collective-permute-done.6.other_ref, f32[512,128]{1,0:T(8,128)} %panel_ref.3, ...), custom_call_target="tpu_custom_call" | custom-call | tf_op jit(solution)/shard_map/pallas_call | solution.py:247
  (13 shorter events, 0.2 us)
Async XLA Ops:
  2.7 1.5 %collective-permute-start = (f32[208,128]{1,0:T(8,128)S(1)}, f32[208,128]{1,0:T(8,128)S(1)}, u32[]{:S(2)}, u32[]{:S(2)}) collective-permute-start(f32[208,128]{1,0:T(8,128)S(1)} %get-tuple-element.11), channel_id=1, source_target_pairs={{0,1},{1,0},{2,3},{3,2},{4,5},{5,4},{6,7},{7,6},{8,9},{9,8},{10,11... | collective-permute-start | bytes 319496 | tf_op jit(solution)/shard_map/ppermute | solution.py:217
  4.2 6.3 %collective-permute-start.1 = (f32[208,128]{1,0:T(8,128)S(1)}, f32[208,128]{1,0:T(8,128)S(1)}, u32[]{:S(2)}, u32[]{:S(2)}) collective-permute-start(f32[208,128]{1,0:T(8,128)S(1)} %pad_maximum_fusion), channel_id=1, source_target_pairs={{0,8},{1,9},{2,10},{3,11},{4,12},{5,13},{6,14},{7,15},{8,0},{9,1},... | collective-permute-start | bytes 319496 | tf_op jit(solution)/shard_map/ppermute | solution.py:217
  10.6 5.9 %collective-permute-start.4 = (f32[208,128]{1,0:T(8,128)S(1)}, f32[208,128]{1,0:T(8,128)S(1)}, u32[]{:S(2)}, u32[]{:S(2)}) collective-permute-start(f32[208,128]{1,0:T(8,128)S(1)} %pad_maximum_fusion.1), channel_id=1, source_target_pairs={{0,6},{1,7},{2,4},{3,5},{4,2},{5,3},{6,0},{7,1},{8,14},{9,15},{10,... | collective-permute-start | bytes 319496 | tf_op jit(solution)/shard_map/ppermute | solution.py:217
  13.2 5.0 %collective-permute-start.3 = (f32[208,128]{1,0:T(8,128)S(1)}, f32[208,128]{1,0:T(8,128)S(1)}, u32[]{:S(2)}, u32[]{:S(2)}) collective-permute-start(f32[208,128]{1,0:T(8,128)S(1)} %pad_maximum_fusion.1), channel_id=1, source_target_pairs={{0,4},{1,5},{2,6},{3,7},{4,0},{5,1},{6,2},{7,3},{8,12},{9,13},{10,... | collective-permute-start | bytes 319496 | tf_op jit(solution)/shard_map/ppermute | solution.py:217
  13.7 4.7 %collective-permute-start.2 = (f32[208,128]{1,0:T(8,128)S(1)}, f32[208,128]{1,0:T(8,128)S(1)}, u32[]{:S(2)}, u32[]{:S(2)}) collective-permute-start(f32[208,128]{1,0:T(8,128)S(1)} %pad_maximum_fusion.1), channel_id=1, source_target_pairs={{0,2},{1,3},{2,0},{3,1},{4,6},{5,7},{6,4},{7,5},{8,10},{9,11},{10,... | collective-permute-start | bytes 319496 | tf_op jit(solution)/shard_map/ppermute | solution.py:217
  18.6 7.2 %collective-permute-start.5 = (f32[208,128]{1,0:T(8,128)S(1)}, f32[208,128]{1,0:T(8,128)S(1)}, u32[]{:S(2)}, u32[]{:S(2)}) collective-permute-start(f32[208,128]{1,0:T(8,128)S(1)} %pad_maximum_fusion.2), channel_id=1, source_target_pairs={{0,16},{1,17},{2,18},{3,19},{4,20},{5,21},{6,22},{7,23},{8,24},{9,... | collective-permute-start | bytes 319496 | tf_op jit(solution)/shard_map/ppermute | solution.py:217
  25.8 1.4 %collective-permute-start.6 = (f32[208,128]{1,0:T(8,128)S(1)}, f32[208,128]{1,0:T(8,128)S(1)}, u32[]{:S(2)}, u32[]{:S(2)}) collective-permute-start(f32[208,128]{1,0:T(8,128)S(1)} %pad_maximum_fusion.3.own_ref), channel_id=1, source_target_pairs={{0,1},{1,0},{2,3},{3,2},{4,5},{5,4},{6,7},{7,6},{8,9},{9,8},{10,11... | collective-permute-start | bytes 319496 | tf_op jit(solution)/shard_map/ppermute | solution.py:217

commit v3 on v2

--- a/solution.py
+++ b/solution.py
@@ -10,15 +10,39 @@
 AXES = ("wide", "narrow")
 SUBLANES = 8
 GRAM_SLICES = 5
-FACTOR_SLICES = 5
+FACTOR_SLICES = 4
+OUTER = 4
+CHUNKS = 4
 VMEM = pl.BlockSpec(memory_space=pltpu.VMEM)
 
 
-def product(left, right, contract=(1, 0)):
-    dims = (((contract[0],), (contract[1],)), ((), ()))
-    return lax.dot_general(
-        left, right, dims, precision=lax.Precision.HIGHEST, preferred_element_type=jnp.float32
-    )
+def matmul(left, right):
+    return exact_product(left, right, (1, 0))
+
+
+def bf16_terms(value, count):
+    terms = []
+    for _ in range(count):
+        term = value.astype(jnp.bfloat16)
+        value = value - term.astype(jnp.float32)
+        terms.append(term)
+    return terms
+
+
+def wide(right):
+    column = jnp.concatenate([right[0], right[1]], 1)
+    return jnp.concatenate([column, column], 0)
+
+
+def product_of_terms(left, right):
+    columns = right[0].shape[1]
+    small = matmul(jnp.concatenate([left[2], left[0]], 1), jnp.concatenate([right[0], right[2]], 0))
+    both = matmul(jnp.concatenate(left[:2], 1), wide(right))
+    return (small + both[:, columns:]) + both[:, :columns]
+
+
+def product(left, right):
+    return product_of_terms(bf16_terms(left, 3), bf16_terms(right, 3))
 
 
 def exact_product(left, right, contract):
@@ -57,7 +81,10 @@
     second, second_low = two_sum(second, second.T)
     high, high_low = two_sum(first, second)
     high, low = two_sum(high, high_low + (second_low + rest))
-    cross = product(panel, trailing_ref[...], (0, 0))
+    dims = (((0,), (0,)), ((), ()))
+    cross = lax.dot_general(
+        panel, trailing_ref[...], dims, precision=lax.Precision.HIGHEST, preferred_element_type=jnp.float32
+    )
     high_half, high_rest = pack_symmetric(high)
     low_half, low_rest = pack_symmetric(low)
     half = high_half.shape[0] // 2
@@ -103,49 +130,74 @@
     return jnp.concatenate([high, low, left[2 * pair_rows :] + right[2 * pair_rows :]], 0)
 
 
+def outer_update(rows, pivots):
+    left, right = bf16_terms(rows, 3), bf16_terms(pivots, 3)
+    left = [left[i] for i in (2, 1, 0, 1, 0, 0)]
+    right = [right[i] for i in (0, 1, 2, 0, 1, 0)]
+    return exact_product(jnp.concatenate(left, 0), jnp.concatenate(right, 0), (0, 0))
+
+
 def factor_and_inverse(tiles):
     count = len(tiles)
     shape = tiles[0].shape
-    lane = lax.broadcasted_iota(jnp.int32, shape, 1)
-    sub = lax.broadcasted_iota(jnp.int32, shape, 0)
+    sub, lane = grid_of(shape)
     over_lanes = lambda v, c: jnp.broadcast_to(v[:, c : c + 1], shape)
     over_rows = lambda v, i: jnp.broadcast_to(v[i : i + 1, :], shape)
     tiles = list(tiles)
     upper, lower = [], []
-    for t in range(count):
-        base = t * SUBLANES
-        current = tiles[t]
-        columns = {
-            s: [over_lanes(tiles[s], base + c) for c in range(SUBLANES)] for s in range(t, count)
-        }
-        inside = (lane >= base) & (lane < base + SUBLANES)
-        for s in range(t + 1, count):
-            tiles[s] = jnp.where(inside, 0.0, tiles[s])
-        pivots = jnp.zeros(shape, jnp.float32)
-        for i in range(SUBLANES):
-            k = base + i
-            pivot = over_rows(columns[t][i], i)
-            inverse = 1.0 / pivot
-            pivots = jnp.where(sub == i, pivot, pivots)
-            row = jnp.where(lane == k, 1.0, over_rows(current, i))
-            later = {c: over_rows(columns[t][c], i) for c in range(i + 1, SUBLANES)}
-            below = jnp.where((lane > k) & (lane < base + SUBLANES), 0.0, row)
-            for s in range(t, count):
-                multiplier = columns[s][i] * inverse
-                if s == t:
-                    if i == SUBLANES - 1:
-                        continue
-                    multiplier = jnp.where(sub > i, multiplier, 0.0)
-                    current = jnp.where((lane == k) & (sub > i), 0.0, current) - multiplier * row
-                else:
-                    tiles[s] = tiles[s] - multiplier * below
-                for c in later:
-                    columns[s][c] = columns[s][c] - multiplier * later[c]
-        scale = lax.rsqrt(pivots)
-        scaled = current * scale
-        diagonal = sub + base
-        upper.append(jnp.where(lane >= diagonal, scaled, 0.0))
-        lower.append(jnp.where(lane < diagonal, scaled, jnp.where(lane == diagonal, scale, 0.0)))
+    for first in range(0, count, OUTER):
+        last = min(first + OUTER, count)
+        size = last - first
+        start, stop = first * SUBLANES, last * SUBLANES
+        columns = [
+            [over_lanes(tiles[first + s], start + c) for c in range(SUBLANES * (s + 1))]
+            for s in range(size)
+        ]
+        pivot_rows = []
+        for t in range(size):
+            base = start + t * SUBLANES
+            current = tiles[first + t]
+            inside = (lane >= base) & (lane < base + SUBLANES)
+            for s in range(t + 1, size):
+                tiles[first + s] = jnp.where(inside, 0.0, tiles[first + s])
+            pivots = jnp.zeros(shape, jnp.float32)
+            for i in range(SUBLANES):
+                k = base + i
+                own = t * SUBLANES + i
+                pivot = over_rows(columns[t][own], i)
+                inverse = 1.0 / pivot
+                pivots = jnp.where(sub == i, pivot, pivots)
+                row = jnp.where(lane == k, 1.0, over_rows(current, i))
+                later = {
+                    c: over_rows(columns[c // SUBLANES][own], c % SUBLANES)
+                    for c in range(own + 1, SUBLANES * size)
+                }
+                if i < SUBLANES - 1:
+                    column = jnp.where(sub > i, columns[t][own], 0.0)
+                    for c in range(own + 1, SUBLANES * (t + 1)):
+                        columns[t][c] = columns[t][c] - (column * later[c]) * inverse
+                    kept = jnp.where((lane == k) & (sub > i), 0.0, current)
+                    current = kept - (column * row) * inverse
+                if t + 1 < size:
+                    below = jnp.where((lane > k) & (lane < base + SUBLANES), 0.0, row) * inverse
+                    scaled = {c: later[c] * inverse for c in later}
+                    for s in range(t + 1, size):
+                        column = columns[s][own]
+                        tiles[first + s] = tiles[first + s] - column * below
+                        for c in range(own + 1, SUBLANES * (s + 1)):
+                            columns[s][c] = columns[s][c] - column * scaled[c]
+            scale = lax.rsqrt(pivots)
+            value = current * scale
+            diagonal = sub + base
+            upper.append(jnp.where(lane >= diagonal, value, 0.0))
+            lower.append(jnp.where(lane < diagonal, value, jnp.where(lane == diagonal, scale, 0.0)))
+            pivot_rows.append(jnp.where(lane >= stop, value, lower[-1]))
+        if last < count:
+            update = outer_update(jnp.concatenate(upper[first:last], 0), jnp.concatenate(pivot_rows, 0))
+            inside = (lane >= start) & (lane < stop)
+            for s in range(last, count):
+                rows = slice(s * SUBLANES, (s + 1) * SUBLANES)
+                tiles[s] = jnp.where(inside, 0.0, tiles[s]) - update[rows]
     return jnp.concatenate(upper, 0), jnp.concatenate(lower, 0)
 
 
@@ -153,8 +205,17 @@
     return [matrix[i : i + SUBLANES] for i in range(0, matrix.shape[0], SUBLANES)]
 
 
-def final_kernel(row_total, core_ref, own_ref, other_ref, panel_ref, trailing_ref, q_ref, r_ref, p_ref, u_ref):
-    order = panel_ref.shape[1]
+def final_kernel(
+    row_total, core_ref, own_ref, other_ref, panel_hbm, trailing_hbm, q_hbm, r_ref, p_ref, u_hbm,
+    panel_ref, trailing_ref, q_ref, u_ref, in_sems, out_sems,
+):
+    copies_in = [
+        pltpu.make_async_copy(panel_hbm, panel_ref, in_sems.at[0]),
+        pltpu.make_async_copy(trailing_hbm, trailing_ref, in_sems.at[1]),
+    ]
+    for copy in copies_in:
+        copy.start()
+    rows, order = panel_ref.shape
     inverse_rows = 1.0 / row_total
     swapped = jnp.full(own_ref.shape, core_ref[0], jnp.int32) != 0
     own = own_ref[...] * inverse_rows
@@ -185,30 +246,38 @@
     for term in orders[3:]:
         rest = rest - term
     remainder = remainder + ((error + error_next) + rest)
-    near_one_t = product(first_inverse_t, first_factor, (1, 1))
-    near_one = product(first_factor, first_inverse_t, (1, 1))
-    carried = product(remainder, first_inverse_t, (1, 1))
+    first_inverse = first_inverse_t.T
+    right = bf16_terms(first_inverse, 3)
+    near_one = product_of_terms(bf16_terms(first_factor, 3), right)
+    carried = product_of_terms(bf16_terms(remainder, 3), right)
     gram_second = product(
-        jnp.concatenate([near_one_t, first_inverse_t], 1), jnp.concatenate([near_one, carried], 0)
+        jnp.concatenate([near_one.T, first_inverse_t], 1), jnp.concatenate([near_one, carried], 0)
     )
     second_factor, second_inverse_t = factor_and_inverse(row_blocks(gram_second))
 
+    inverse_t = product(second_inverse_t, first_inverse_t)
+    inverse = bf16_terms(inverse_t.T, 3)
+    projection = product(inverse_t, cross)
+    near_projection = wide(bf16_terms(projection, 2))
+    p_ref[...] = projection
     r_ref[...] = product(second_factor, first_factor)
-    inverse_t = product(second_inverse_t, first_inverse_t)
-    projection = product(inverse_t, cross)
-    p_ref[...] = projection
-    q_factor = product(panel_ref[...], inverse_t, (1, 1))
-    q_ref[...] = q_factor
-    u_ref[...] = trailing_ref[...] - product(q_factor, projection)
-
-
-def call(body, outs, n_in, specs=None, near=False):
-    return pl.pallas_call(
-        body,
-        out_shape=[(pltpu.VMEM if near else jax.ShapeDtypeStruct)(shape, jnp.float32) for shape in outs],
-        in_specs=specs or [VMEM] * n_in,
-        out_specs=[VMEM] * len(outs),
-    )
+    for copy in copies_in:
+        copy.wait()
+    copies_out = []
+    depth = rows // CHUNKS
+    width = projection.shape[1]
+    for chunk in range(CHUNKS):
+        at = pl.ds(chunk * depth, depth)
+        q_factor = product_of_terms(bf16_terms(panel_ref[at, :], 3), inverse)
+        q_ref[at, :] = q_factor
+        copies_out.append(pltpu.make_async_copy(q_ref.at[at, :], q_hbm.at[at, :], out_sems.at[0, chunk]))
+        copies_out[-1].start()
+        both = matmul(jnp.concatenate(bf16_terms(q_factor, 2), 1), near_projection)
+        u_ref[at, :] = trailing_ref[at, :] - (both[:, width:] + both[:, :width])
+        copies_out.append(pltpu.make_async_copy(u_ref.at[at, :], u_hbm.at[at, :], out_sems.at[1, chunk]))
+        copies_out[-1].start()
+    for copy in copies_out:
+        copy.wait()
 
 
 def all_sum(blocks, pair_rows):
@@ -237,14 +306,32 @@
     width = trailing.shape[1]
     row_total = float(rows * lax.axis_size(AXES))
     pair_rows = order // 4 + SUBLANES
-    (local,) = call(gram_kernel, [(2, 2 * pair_rows + order, order)], 2, near=True)(panel, trailing)
+    local = pl.pallas_call(
+        gram_kernel,
+        out_shape=pltpu.VMEM((2, 2 * pair_rows + order, order), jnp.float32),
+        in_specs=[VMEM] * 2,
+        out_specs=VMEM,
+    )(panel, trailing)
     own, other, odd = all_sum(local, pair_rows)
-    outs = [(rows, order), (order, order), (order, width), (rows, width)]
-    specs = [pl.BlockSpec(memory_space=pltpu.SMEM)] + [VMEM] * 4
-    body = functools.partial(final_kernel, row_total)
     own, other = [pltpu.with_memory_space_constraint(v, pltpu.VMEM) for v in (own, other)]
-    core = odd.astype(jnp.int32).reshape(1)
-    return tuple(call(body, outs, 5, specs)(core, own, other, panel, trailing))
+    shapes = [(rows, order), (order, order), (order, width), (rows, width)]
+    far = pl.BlockSpec(memory_space=pltpu.HBM)
+    return tuple(
+        pl.pallas_call(
+            functools.partial(final_kernel, row_total),
+            out_shape=[jax.ShapeDtypeStruct(shape, jnp.float32) for shape in shapes],
+            in_specs=[pl.BlockSpec(memory_space=pltpu.SMEM), VMEM, VMEM, far, far],
+            out_specs=[far, VMEM, VMEM, far],
+            scratch_shapes=[
+                pltpu.VMEM((rows, order), jnp.float32),
+                pltpu.VMEM((rows, width), jnp.float32),
+                pltpu.VMEM((rows, order), jnp.float32),
+                pltpu.VMEM((rows, width), jnp.float32),
+                pltpu.SemaphoreType.DMA((2,)),
+                pltpu.SemaphoreType.DMA((2, CHUNKS)),
+            ],
+        )(odd.astype(jnp.int32).reshape(1), own, other, panel, trailing)
+    )
 
 
 def solution(mesh):

time: 40.1 us -> 37.6 us (0.938)
  Pallas kernels: 14.7 us -> 12.2 us
    pallas_call x2, Pallas kernels: 14.7 us -> 12.2 us  [the longest x1 10.2 us: on_device(): pl.pallas_call(functools.partial(final_kernel, row_total), out_shape=[jax...]
where the time goes in v3:
time: 37.6 us; the launch traced here: 37.4 us
  waiting for transfers between devices  14.5 us (39%)
  Pallas kernels  12.2 us (32%)
  starting transfers between devices  9.82 us (26%)
  between operations  0.74 us (2%)
    ppermute x7, waiting for transfers between devices, all_sum(): lax.ppermute(value, AXES, [(i, i ^ mask) for i in range(devices)])  14.5 us
    pallas_call x1, Pallas kernels, on_device(): pl.pallas_call(functools.partial(final_kernel, row_total), out_shape=[jax...  10.2 us
    ppermute x7, starting transfers between devices, all_sum(): lax.ppermute(value, AXES, [(i, i ^ mask) for i in range(devices)])  9.82 us
    pallas_call x1, Pallas kernels, on_device(): pl.pallas_call(gram_kernel, out_shape=pltpu.VMEM((2, 2 * pair_rows + orde...  2 us
  transfers between devices with their start and end apart: 7, of which 7 were waited for; matrix products, arithmetic and copies ran while one was open for 0% of the time, Pallas kernels for 0%

profile of v3, /device:TPU:0, one launch (start us, length us, event | category | flops | bytes accessed | tf_op | source)
XLA Modules:
  0.0 37.4 jit_solution(14477876080703446504)
XLA Ops:
  0.6 2.0 %shard_map.57 = f32[2,208,128]{2,1,0:T(8,128)S(1)} custom-call(f32[512,128]{1,0:T(8,128)} %panel_hbm.1, f32[512,256]{1,0:T(8,128)} %trailing_hbm.1), custom_call_target="tpu_custom_call" | custom-call | tf_op jit(solution)/shard_map/pallas_call | solution.py:309
  2.7 0.6 %collective-permute-start = (f32[208,128]{1,0:T(8,128)S(1)}, f32[208,128]{1,0:T(8,128)S(1)}, u32[]{:S(2)}, u32[]{:S(2)}) collective-permute-start(f32[208,128]{1,0:T(8,128)S(1)} %get-tuple-element.11), channel_id=1, source_target_pairs={{0,1},{1,0},{2,3},{3,2},{4,5},{5,4},{6,7},{7,6},{8,9},{9,8},{10,11... | collective-permute-start | bytes 319496 | tf_op jit(solution)/shard_map/ppermute | solution.py:286
  3.2 1.0 %collective-permute-done = f32[208,128]{1,0:T(8,128)S(1)} collective-permute-done((f32[208,128]{1,0:T(8,128)S(1)}, f32[208,128]{1,0:T(8,128)S(1)}, u32[]{:S(2)}, u32[]{:S(2)}) %collective-permute-start) | collective-permute-done | bytes 106528 | tf_op jit(solution)/shard_map/ppermute | solution.py:286
  4.2 3.0 %collective-permute-start.1 = (f32[208,128]{1,0:T(8,128)S(1)}, f32[208,128]{1,0:T(8,128)S(1)}, u32[]{:S(2)}, u32[]{:S(2)}) collective-permute-start(f32[208,128]{1,0:T(8,128)S(1)} %pad_maximum_fusion), channel_id=1, source_target_pairs={{0,8},{1,9},{2,10},{3,11},{4,12},{5,13},{6,14},{7,15},{8,0},{9,1},... | collective-permute-start | bytes 319496 | tf_op jit(solution)/shard_map/ppermute | solution.py:286
  7.2 3.3 %collective-permute-done.1 = f32[208,128]{1,0:T(8,128)S(1)} collective-permute-done((f32[208,128]{1,0:T(8,128)S(1)}, f32[208,128]{1,0:T(8,128)S(1)}, u32[]{:S(2)}, u32[]{:S(2)}) %collective-permute-start.1) | collective-permute-done | bytes 106528 | tf_op jit(solution)/shard_map/ppermute | solution.py:286
  10.6 2.7 %collective-permute-start.4 = (f32[208,128]{1,0:T(8,128)S(1)}, f32[208,128]{1,0:T(8,128)S(1)}, u32[]{:S(2)}, u32[]{:S(2)}) collective-permute-start(f32[208,128]{1,0:T(8,128)S(1)} %pad_maximum_fusion.1), channel_id=1, source_target_pairs={{0,6},{1,7},{2,4},{3,5},{4,2},{5,3},{6,0},{7,1},{8,14},{9,15},{10,... | collective-permute-start | bytes 319496 | tf_op jit(solution)/shard_map/ppermute | solution.py:286
  13.2 0.5 %collective-permute-start.3 = (f32[208,128]{1,0:T(8,128)S(1)}, f32[208,128]{1,0:T(8,128)S(1)}, u32[]{:S(2)}, u32[]{:S(2)}) collective-permute-start(f32[208,128]{1,0:T(8,128)S(1)} %pad_maximum_fusion.1), channel_id=1, source_target_pairs={{0,4},{1,5},{2,6},{3,7},{4,0},{5,1},{6,2},{7,3},{8,12},{9,13},{10,... | collective-permute-start | bytes 319496 | tf_op jit(solution)/shard_map/ppermute | solution.py:286
  13.7 0.4 collective-permute-start.2
  14.1 2.3 %collective-permute-done.4 = f32[208,128]{1,0:T(8,128)S(1)} collective-permute-done((f32[208,128]{1,0:T(8,128)S(1)}, f32[208,128]{1,0:T(8,128)S(1)}, u32[]{:S(2)}, u32[]{:S(2)}) %collective-permute-start.4) | collective-permute-done | bytes 106528 | tf_op jit(solution)/shard_map/ppermute | solution.py:286
  16.4 1.8 %collective-permute-done.3 = f32[208,128]{1,0:T(8,128)S(1)} collective-permute-done((f32[208,128]{1,0:T(8,128)S(1)}, f32[208,128]{1,0:T(8,128)S(1)}, u32[]{:S(2)}, u32[]{:S(2)}) %collective-permute-start.3) | collective-permute-done | bytes 106528 | tf_op jit(solution)/shard_map/ppermute | solution.py:286
  18.3 0.2 collective-permute-done.2
  18.6 2.7 %collective-permute-start.5 = (f32[208,128]{1,0:T(8,128)S(1)}, f32[208,128]{1,0:T(8,128)S(1)}, u32[]{:S(2)}, u32[]{:S(2)}) collective-permute-start(f32[208,128]{1,0:T(8,128)S(1)} %pad_maximum_fusion.2), channel_id=1, source_target_pairs={{0,16},{1,17},{2,18},{3,19},{4,20},{5,21},{6,22},{7,23},{8,24},{9,... | collective-permute-start | bytes 319496 | tf_op jit(solution)/shard_map/ppermute | solution.py:286
  21.2 4.5 %collective-permute-done.5 = f32[208,128]{1,0:T(8,128)S(1)} collective-permute-done((f32[208,128]{1,0:T(8,128)S(1)}, f32[208,128]{1,0:T(8,128)S(1)}, u32[]{:S(2)}, u32[]{:S(2)}) %collective-permute-start.5) | collective-permute-done | bytes 106528 | tf_op jit(solution)/shard_map/ppermute | solution.py:286
  25.8 0.1 collective-permute-start.6
  25.9 1.3 %collective-permute-done.6.other_ref = f32[208,128]{1,0:T(8,128)S(1)} collective-permute-done((f32[208,128]{1,0:T(8,128)S(1)}, f32[208,128]{1,0:T(8,128)S(1)}, u32[]{:S(2)}, u32[]{:S(2)}) %collective-permute-start.6) | collective-permute-done | bytes 106528 | tf_op jit(solution)/shard_map/ppermute | solution.py:286
  27.2 10.2 %shard_map.58 = (f32[512,128]{1,0:T(8,128)}, f32[128,128]{1,0:T(8,128)}, f32[128,256]{1,0:T(8,128)}, f32[512,256]{1,0:T(8,128)}) custom-call(s32[1]{0:T(128)} %bitcast.core_ref, f32[208,128]{1,0:T(8,128)S(1)} %pad_maximum_fusion.3.own_ref, f32[208,128]{1,0:T(8,128)S(1)} %collective-permute-done.6.other_ref, f32[512,128]{1,0:T(8,128)} %panel_hbm.1, ...), custom_call_target="tpu_custom_call" | custom-call | tf_op jit(solution)/shard_map/pallas_call | solution.py:320
  (13 shorter events, 0.2 us)
Async XLA Ops:
  2.7 1.5 %collective-permute-start = (f32[208,128]{1,0:T(8,128)S(1)}, f32[208,128]{1,0:T(8,128)S(1)}, u32[]{:S(2)}, u32[]{:S(2)}) collective-permute-start(f32[208,128]{1,0:T(8,128)S(1)} %get-tuple-element.11), channel_id=1, source_target_pairs={{0,1},{1,0},{2,3},{3,2},{4,5},{5,4},{6,7},{7,6},{8,9},{9,8},{10,11... | collective-permute-start | bytes 319496 | tf_op jit(solution)/shard_map/ppermute | solution.py:286
  4.2 6.3 %collective-permute-start.1 = (f32[208,128]{1,0:T(8,128)S(1)}, f32[208,128]{1,0:T(8,128)S(1)}, u32[]{:S(2)}, u32[]{:S(2)}) collective-permute-start(f32[208,128]{1,0:T(8,128)S(1)} %pad_maximum_fusion), channel_id=1, source_target_pairs={{0,8},{1,9},{2,10},{3,11},{4,12},{5,13},{6,14},{7,15},{8,0},{9,1},... | collective-permute-start | bytes 319496 | tf_op jit(solution)/shard_map/ppermute | solution.py:286
  10.6 5.9 %collective-permute-start.4 = (f32[208,128]{1,0:T(8,128)S(1)}, f32[208,128]{1,0:T(8,128)S(1)}, u32[]{:S(2)}, u32[]{:S(2)}) collective-permute-start(f32[208,128]{1,0:T(8,128)S(1)} %pad_maximum_fusion.1), channel_id=1, source_target_pairs={{0,6},{1,7},{2,4},{3,5},{4,2},{5,3},{6,0},{7,1},{8,14},{9,15},{10,... | collective-permute-start | bytes 319496 | tf_op jit(solution)/shard_map/ppermute | solution.py:286
  13.2 5.0 %collective-permute-start.3 = (f32[208,128]{1,0:T(8,128)S(1)}, f32[208,128]{1,0:T(8,128)S(1)}, u32[]{:S(2)}, u32[]{:S(2)}) collective-permute-start(f32[208,128]{1,0:T(8,128)S(1)} %pad_maximum_fusion.1), channel_id=1, source_target_pairs={{0,4},{1,5},{2,6},{3,7},{4,0},{5,1},{6,2},{7,3},{8,12},{9,13},{10,... | collective-permute-start | bytes 319496 | tf_op jit(solution)/shard_map/ppermute | solution.py:286
  13.7 4.7 %collective-permute-start.2 = (f32[208,128]{1,0:T(8,128)S(1)}, f32[208,128]{1,0:T(8,128)S(1)}, u32[]{:S(2)}, u32[]{:S(2)}) collective-permute-start(f32[208,128]{1,0:T(8,128)S(1)} %pad_maximum_fusion.1), channel_id=1, source_target_pairs={{0,2},{1,3},{2,0},{3,1},{4,6},{5,7},{6,4},{7,5},{8,10},{9,11},{10,... | collective-permute-start | bytes 319496 | tf_op jit(solution)/shard_map/ppermute | solution.py:286
  18.6 7.2 %collective-permute-start.5 = (f32[208,128]{1,0:T(8,128)S(1)}, f32[208,128]{1,0:T(8,128)S(1)}, u32[]{:S(2)}, u32[]{:S(2)}) collective-permute-start(f32[208,128]{1,0:T(8,128)S(1)} %pad_maximum_fusion.2), channel_id=1, source_target_pairs={{0,16},{1,17},{2,18},{3,19},{4,20},{5,21},{6,22},{7,23},{8,24},{9,... | collective-permute-start | bytes 319496 | tf_op jit(solution)/shard_map/ppermute | solution.py:286
  25.8 1.4 %collective-permute-start.6 = (f32[208,128]{1,0:T(8,128)S(1)}, f32[208,128]{1,0:T(8,128)S(1)}, u32[]{:S(2)}, u32[]{:S(2)}) collective-permute-start(f32[208,128]{1,0:T(8,128)S(1)} %pad_maximum_fusion.3.own_ref), channel_id=1, source_target_pairs={{0,1},{1,0},{2,3},{3,2},{4,5},{5,4},{6,7},{7,6},{8,9},{9,8},{10,11... | collective-permute-start | bytes 319496 | tf_op jit(solution)/shard_map/ppermute | solution.py:286

commit v4 on v3

--- a/solution.py
+++ b/solution.py
@@ -69,34 +69,35 @@
 
 def gram_kernel(panel_ref, trailing_ref, out_ref):
     panel = panel_ref[...]
+    order = panel.shape[1]
     peak = jnp.max(jnp.abs(panel), axis=0, keepdims=True)
     terms = fixed_point_slices(panel, peak, 7, GRAM_SLICES)
-    dot = functools.partial(exact_product, contract=(0, 0))
-    first = dot(terms[0], terms[0])
-    second = dot(terms[0], terms[1])
-    rest = dot(terms[0], terms[2])
-    rest = rest + dot(terms[1], terms[2]) + dot(terms[0], terms[3])
-    rest = rest + dot(terms[0], terms[4]) + dot(terms[1], terms[3])
-    rest = rest + rest.T + dot(terms[1], terms[1]) + dot(terms[2], terms[2])
-    second, second_low = two_sum(second, second.T)
-    high, high_low = two_sum(first, second)
+    others = bf16_terms(trailing_ref[...], 3)
+    width = others[0].shape[1]
+    wide_product = lambda left, right: exact_product(left, jnp.concatenate(right, 1), (0, 0))
+    zero = wide_product(terms[0], terms + others)
+    one = wide_product(terms[1], terms[1:4] + others[:2])
+    two = wide_product(terms[2], terms[2:3] + others[:1])
+    block = lambda value, i: value[:, i * order : (i + 1) * order]
+    rest = (block(zero, 2) + block(one, 1)) + (block(zero, 3) + (block(zero, 4) + block(one, 2)))
+    rest = (rest + rest.T) + (block(one, 0) + block(two, 0))
+    second, second_low = two_sum(block(zero, 1), block(zero, 1).T)
+    high, high_low = two_sum(block(zero, 0), second)
     high, low = two_sum(high, high_low + (second_low + rest))
-    dims = (((0,), (0,)), ((), ()))
-    cross = lax.dot_general(
-        panel, trailing_ref[...], dims, precision=lax.Precision.HIGHEST, preferred_element_type=jnp.float32
-    )
+    part = lambda value, at, i: value[:, at * order + i * width : at * order + (i + 1) * width]
+    cross = (part(two, 1, 0) + part(one, 3, 1)) + part(zero, GRAM_SLICES, 2)
+    cross = (cross + (part(one, 3, 0) + part(zero, GRAM_SLICES, 1))) + part(zero, GRAM_SLICES, 0)
     high_half, high_rest = pack_symmetric(high)
     low_half, low_rest = pack_symmetric(low)
     half = high_half.shape[0] // 2
-    width = cross.shape[1] // 2
     for core in range(2):
         rows = slice(core * half, (core + 1) * half)
-        blocks = [high_half[rows], high_rest, low_half[rows], low_rest]
-        blocks.append(cross[:, core * width : (core + 1) * width])
+        blocks = [high_half[rows], low_half[rows]]
+        blocks += [cross[:, core * width // 2 : (core + 1) * width // 2], high_rest[:1], low_rest[:1]]
         at = 0
-        for block in blocks:
-            out_ref[core, at : at + block.shape[0], :] = block
-            at += block.shape[0]
+        for value in blocks:
+            out_ref[core, at : at + value.shape[0], :] = value
+            at += value.shape[0]
 
 
 def grid_of(shape):
@@ -127,17 +128,19 @@
 def add_terms(left, right, pair_rows):
     high, error = two_sum(left[:pair_rows], right[:pair_rows])
     low = (left[pair_rows : 2 * pair_rows] + right[pair_rows : 2 * pair_rows]) + error
-    return jnp.concatenate([high, low, left[2 * pair_rows :] + right[2 * pair_rows :]], 0)
-
-
-def outer_update(rows, pivots):
+    plain = left[2 * pair_rows : -2] + right[2 * pair_rows : -2]
+    rest, error = two_sum(left[-2:-1], right[-2:-1])
+    return jnp.concatenate([high, low, plain, rest, (left[-1:] + right[-1:]) + error], 0)
+
+
+def outer_update(rows, pivots, first):
     left, right = bf16_terms(rows, 3), bf16_terms(pivots, 3)
     left = [left[i] for i in (2, 1, 0, 1, 0, 0)]
     right = [right[i] for i in (0, 1, 2, 0, 1, 0)]
-    return exact_product(jnp.concatenate(left, 0), jnp.concatenate(right, 0), (0, 0))
-
-
-def factor_and_inverse(tiles):
+    return matmul(jnp.concatenate(left, 0).T[first:], jnp.concatenate(right, 0))
+
+
+def factor_and_inverse(tiles, finished=lambda rows: None):
     count = len(tiles)
     shape = tiles[0].shape
     sub, lane = grid_of(shape)
@@ -173,31 +176,31 @@
                     for c in range(own + 1, SUBLANES * size)
                 }
                 if i < SUBLANES - 1:
-                    column = jnp.where(sub > i, columns[t][own], 0.0)
+                    column = jnp.where(sub > i, columns[t][own], 0.0) * inverse
                     for c in range(own + 1, SUBLANES * (t + 1)):
-                        columns[t][c] = columns[t][c] - (column * later[c]) * inverse
-                    kept = jnp.where((lane == k) & (sub > i), 0.0, current)
-                    current = kept - (column * row) * inverse
+                        columns[t][c] = columns[t][c] - column * later[c]
+                    current = jnp.where((lane == k) & (sub > i), 0.0, current) - column * row
                 if t + 1 < size:
-                    below = jnp.where((lane > k) & (lane < base + SUBLANES), 0.0, row) * inverse
-                    scaled = {c: later[c] * inverse for c in later}
+                    below = jnp.where((lane > k) & (lane < base + SUBLANES), 0.0, row)
                     for s in range(t + 1, size):
-                        column = columns[s][own]
+                        column = columns[s][own] * inverse
                         tiles[first + s] = tiles[first + s] - column * below
                         for c in range(own + 1, SUBLANES * (s + 1)):
-                            columns[s][c] = columns[s][c] - column * scaled[c]
+                            columns[s][c] = columns[s][c] - column * later[c]
             scale = lax.rsqrt(pivots)
             value = current * scale
             diagonal = sub + base
             upper.append(jnp.where(lane >= diagonal, value, 0.0))
             lower.append(jnp.where(lane < diagonal, value, jnp.where(lane == diagonal, scale, 0.0)))
             pivot_rows.append(jnp.where(lane >= stop, value, lower[-1]))
+        finished(jnp.concatenate(upper[first:last], 0))
         if last < count:
-            update = outer_update(jnp.concatenate(upper[first:last], 0), jnp.concatenate(pivot_rows, 0))
+            rows = jnp.concatenate(upper[first:last], 0)
+            update = outer_update(rows, jnp.concatenate(pivot_rows, 0), stop)
             inside = (lane >= start) & (lane < stop)
             for s in range(last, count):
-                rows = slice(s * SUBLANES, (s + 1) * SUBLANES)
-                tiles[s] = jnp.where(inside, 0.0, tiles[s]) - update[rows]
+                at = (s - last) * SUBLANES
+                tiles[s] = jnp.where(inside, 0.0, tiles[s]) - update[at : at + SUBLANES]
     return jnp.concatenate(upper, 0), jnp.concatenate(lower, 0)
 
 
@@ -222,24 +225,28 @@
     other = other_ref[...] * inverse_rows
     halves = [jnp.where(swapped, other, own), jnp.where(swapped, own, other)]
     quarter = order // 4
-    pair_rows = quarter + SUBLANES
-    pick = lambda at: unpack_symmetric(
+    pick = lambda at, row: unpack_symmetric(
         jnp.concatenate([half[at : at + quarter] for half in halves], 0),
-        halves[0][at + quarter : at + pair_rows],
+        halves[0][row : row + 1],
     )
-    high = pick(0)
-    low = pick(pair_rows)
-    cross = jnp.concatenate([half[2 * pair_rows :] for half in halves], 1)
-    high_tiles = row_blocks(high)
-    first_factor, first_inverse_t = factor_and_inverse(high_tiles)
-
-    peak = jnp.max(jnp.abs(first_factor), axis=0, keepdims=True)
-    terms = fixed_point_slices(first_factor, peak, 8, FACTOR_SLICES)
-    orders = []
-    for size in range(1, FACTOR_SLICES + 1):
-        left = jnp.concatenate(terms[:size], 0)
-        right = jnp.concatenate(terms[:size][::-1], 0)
-        orders.append(exact_product(left, right, (0, 0)))
+    high = pick(0, own_ref.shape[0] - 2)
+    low = pick(quarter, own_ref.shape[0] - 1)
+    cross = jnp.concatenate([half[2 * quarter : -2] for half in halves], 1)
+
+    row, lane = grid_of(high.shape)
+    peak = jnp.sqrt(jnp.sum(jnp.where(row == lane, high, 0.0), axis=0, keepdims=True)) * 1.001
+    orders = [None] * FACTOR_SLICES
+
+    def add_products(rows):
+        terms = fixed_point_slices(rows, peak, 8, FACTOR_SLICES)
+        for size in range(1, FACTOR_SLICES + 1):
+            left = jnp.concatenate(terms[:size], 0)
+            right = jnp.concatenate(terms[:size][::-1], 0)
+            value = exact_product(left, right, (0, 0))
+            orders[size - 1] = value if orders[size - 1] is None else orders[size - 1] + value
+
+    first_factor, first_inverse_t = factor_and_inverse(row_blocks(high), add_products)
+
     remainder, error = two_sum(high, -orders[0])
     remainder, error_next = two_sum(remainder, -orders[1])
     rest = low - orders[2]
@@ -305,10 +312,10 @@
     rows, order = panel.shape
     width = trailing.shape[1]
     row_total = float(rows * lax.axis_size(AXES))
-    pair_rows = order // 4 + SUBLANES
+    pair_rows = order // 4
     local = pl.pallas_call(
         gram_kernel,
-        out_shape=pltpu.VMEM((2, 2 * pair_rows + order, order), jnp.float32),
+        out_shape=pltpu.VMEM((2, 2 * pair_rows + order + 2, order), jnp.float32),
         in_specs=[VMEM] * 2,
         out_specs=VMEM,
     )(panel, trailing)

time: 37.6 us -> 36.9 us (0.981)
  waiting for transfers between devices: 14.5 us -> 14 us
    ppermute x7, waiting for transfers between devices: 14.5 us -> 14 us  [all_sum(): lax.ppermute(value, AXES, [(i, i ^ mask) for i in range(devices)])]
where the time goes in v4:
time: 36.9 us; the launch traced here: 36.7 us
  waiting for transfers between devices  14 us (38%)
  Pallas kernels  11.9 us (32%)
  starting transfers between devices  9.79 us (27%)
  between operations  0.73 us (2%)
    ppermute x7, waiting for transfers between devices, all_sum(): lax.ppermute(value, AXES, [(i, i ^ mask) for i in range(devices)])  14 us
    pallas_call x1, Pallas kernels, on_device(): pl.pallas_call(functools.partial(final_kernel, row_total), out_shape=[jax...  9.95 us
    ppermute x7, starting transfers between devices, all_sum(): lax.ppermute(value, AXES, [(i, i ^ mask) for i in range(devices)])  9.79 us
    pallas_call x1, Pallas kernels, on_device(): pl.pallas_call(gram_kernel, out_shape=pltpu.VMEM((2, 2 * pair_rows + orde...  1.94 us
  transfers between devices with their start and end apart: 7, of which 7 were waited for; matrix products, arithmetic and copies ran while one was open for 0% of the time, Pallas kernels for 0%

profile of v4, /device:TPU:0, one launch (start us, length us, event | category | flops | bytes accessed | tf_op | source)
XLA Modules:
  0.0 36.7 jit_solution(3412023234185095411)
XLA Ops:
  0.6 1.9 %shard_map.57 = f32[2,194,128]{2,1,0:T(8,128)S(1)} custom-call(f32[512,128]{1,0:T(8,128)} %panel_hbm.1, f32[512,256]{1,0:T(8,128)} %trailing_hbm.1), custom_call_target="tpu_custom_call" | custom-call | tf_op jit(solution)/shard_map/pallas_call | solution.py:316
  2.6 0.6 %collective-permute-start = (f32[194,128]{1,0:T(8,128)S(1)}, f32[194,128]{1,0:T(8,128)S(1)}, u32[]{:S(2)}, u32[]{:S(2)}) collective-permute-start(f32[194,128]{1,0:T(8,128)S(1)} %get-tuple-element.17), channel_id=1, source_target_pairs={{0,1},{1,0},{2,3},{3,2},{4,5},{5,4},{6,7},{7,6},{8,9},{9,8},{10,11... | collective-permute-start | bytes 297992 | tf_op jit(solution)/shard_map/ppermute | solution.py:293
  3.2 0.9 %collective-permute-done = f32[194,128]{1,0:T(8,128)S(1)} collective-permute-done((f32[194,128]{1,0:T(8,128)S(1)}, f32[194,128]{1,0:T(8,128)S(1)}, u32[]{:S(2)}, u32[]{:S(2)}) %collective-permute-start) | collective-permute-done | bytes 99360 | tf_op jit(solution)/shard_map/ppermute | solution.py:293
  4.2 3.0 %collective-permute-start.1 = (f32[194,128]{1,0:T(8,128)S(1)}, f32[194,128]{1,0:T(8,128)S(1)}, u32[]{:S(2)}, u32[]{:S(2)}) collective-permute-start(f32[194,128]{1,0:T(8,128)S(1)} %concatenate.12), channel_id=1, source_target_pairs={{0,8},{1,9},{2,10},{3,11},{4,12},{5,13},{6,14},{7,15},{8,0},{9,1},... | collective-permute-start | bytes 297992 | tf_op jit(solution)/shard_map/ppermute | solution.py:293
  7.2 3.2 %collective-permute-done.1 = f32[194,128]{1,0:T(8,128)S(1)} collective-permute-done((f32[194,128]{1,0:T(8,128)S(1)}, f32[194,128]{1,0:T(8,128)S(1)}, u32[]{:S(2)}, u32[]{:S(2)}) %collective-permute-start.1) | collective-permute-done | bytes 99360 | tf_op jit(solution)/shard_map/ppermute | solution.py:293
  10.5 2.7 %collective-permute-start.4 = (f32[194,128]{1,0:T(8,128)S(1)}, f32[194,128]{1,0:T(8,128)S(1)}, u32[]{:S(2)}, u32[]{:S(2)}) collective-permute-start(f32[194,128]{1,0:T(8,128)S(1)} %concatenate.13), channel_id=1, source_target_pairs={{0,6},{1,7},{2,4},{3,5},{4,2},{5,3},{6,0},{7,1},{8,14},{9,15},{10,... | collective-permute-start | bytes 297992 | tf_op jit(solution)/shard_map/ppermute | solution.py:293
  13.1 0.5 %collective-permute-start.3 = (f32[194,128]{1,0:T(8,128)S(1)}, f32[194,128]{1,0:T(8,128)S(1)}, u32[]{:S(2)}, u32[]{:S(2)}) collective-permute-start(f32[194,128]{1,0:T(8,128)S(1)} %concatenate.13), channel_id=1, source_target_pairs={{0,4},{1,5},{2,6},{3,7},{4,0},{5,1},{6,2},{7,3},{8,12},{9,13},{10,... | collective-permute-start | bytes 297992 | tf_op jit(solution)/shard_map/ppermute | solution.py:293
  13.6 0.4 %collective-permute-start.2 = (f32[194,128]{1,0:T(8,128)S(1)}, f32[194,128]{1,0:T(8,128)S(1)}, u32[]{:S(2)}, u32[]{:S(2)}) collective-permute-start(f32[194,128]{1,0:T(8,128)S(1)} %concatenate.13), channel_id=1, source_target_pairs={{0,2},{1,3},{2,0},{3,1},{4,6},{5,7},{6,4},{7,5},{8,10},{9,11},{10,... | collective-permute-start | bytes 297992 | tf_op jit(solution)/shard_map/ppermute | solution.py:293
  14.0 2.2 %collective-permute-done.4 = f32[194,128]{1,0:T(8,128)S(1)} collective-permute-done((f32[194,128]{1,0:T(8,128)S(1)}, f32[194,128]{1,0:T(8,128)S(1)}, u32[]{:S(2)}, u32[]{:S(2)}) %collective-permute-start.4) | collective-permute-done | bytes 99360 | tf_op jit(solution)/shard_map/ppermute | solution.py:293
  16.2 1.8 %collective-permute-done.3 = f32[194,128]{1,0:T(8,128)S(1)} collective-permute-done((f32[194,128]{1,0:T(8,128)S(1)}, f32[194,128]{1,0:T(8,128)S(1)}, u32[]{:S(2)}, u32[]{:S(2)}) %collective-permute-start.3) | collective-permute-done | bytes 99360 | tf_op jit(solution)/shard_map/ppermute | solution.py:293
  18.0 0.3 collective-permute-done.2
  18.4 2.6 %collective-permute-start.5 = (f32[194,128]{1,0:T(8,128)S(1)}, f32[194,128]{1,0:T(8,128)S(1)}, u32[]{:S(2)}, u32[]{:S(2)}) collective-permute-start(f32[194,128]{1,0:T(8,128)S(1)} %concatenate.14), channel_id=1, source_target_pairs={{0,16},{1,17},{2,18},{3,19},{4,20},{5,21},{6,22},{7,23},{8,24},{9,... | collective-permute-start | bytes 297992 | tf_op jit(solution)/shard_map/ppermute | solution.py:293
  21.0 4.3 %collective-permute-done.5 = f32[194,128]{1,0:T(8,128)S(1)} collective-permute-done((f32[194,128]{1,0:T(8,128)S(1)}, f32[194,128]{1,0:T(8,128)S(1)}, u32[]{:S(2)}, u32[]{:S(2)}) %collective-permute-start.5) | collective-permute-done | bytes 99360 | tf_op jit(solution)/shard_map/ppermute | solution.py:293
  25.4 0.1 collective-permute-start.6
  25.5 1.3 %collective-permute-done.6.other_ref = f32[194,128]{1,0:T(8,128)S(1)} collective-permute-done((f32[194,128]{1,0:T(8,128)S(1)}, f32[194,128]{1,0:T(8,128)S(1)}, u32[]{:S(2)}, u32[]{:S(2)}) %collective-permute-start.6) | collective-permute-done | bytes 99360 | tf_op jit(solution)/shard_map/ppermute | solution.py:293
  26.8 10.0 %shard_map.58 = (f32[512,128]{1,0:T(8,128)}, f32[128,128]{1,0:T(8,128)}, f32[128,256]{1,0:T(8,128)}, f32[512,256]{1,0:T(8,128)}) custom-call(s32[1]{0:T(128)} %bitcast.core_ref, f32[194,128]{1,0:T(8,128)S(1)} %concatenate.15.own_ref, f32[194,128]{1,0:T(8,128)S(1)} %collective-permute-done.6.other_ref, f32[512,128]{1,0:T(8,128)} %panel_hbm.1, ...), custom_call_target="tpu_custom_call" | custom-call | tf_op jit(solution)/shard_map/pallas_call | solution.py:327
  (17 shorter events, 0.3 us)
Async XLA Ops:
  2.6 1.5 %collective-permute-start = (f32[194,128]{1,0:T(8,128)S(1)}, f32[194,128]{1,0:T(8,128)S(1)}, u32[]{:S(2)}, u32[]{:S(2)}) collective-permute-start(f32[194,128]{1,0:T(8,128)S(1)} %get-tuple-element.17), channel_id=1, source_target_pairs={{0,1},{1,0},{2,3},{3,2},{4,5},{5,4},{6,7},{7,6},{8,9},{9,8},{10,11... | collective-permute-start | bytes 297992 | tf_op jit(solution)/shard_map/ppermute | solution.py:293
  4.2 6.2 %collective-permute-start.1 = (f32[194,128]{1,0:T(8,128)S(1)}, f32[194,128]{1,0:T(8,128)S(1)}, u32[]{:S(2)}, u32[]{:S(2)}) collective-permute-start(f32[194,128]{1,0:T(8,128)S(1)} %concatenate.12), channel_id=1, source_target_pairs={{0,8},{1,9},{2,10},{3,11},{4,12},{5,13},{6,14},{7,15},{8,0},{9,1},... | collective-permute-start | bytes 297992 | tf_op jit(solution)/shard_map/ppermute | solution.py:293
  10.5 5.8 %collective-permute-start.4 = (f32[194,128]{1,0:T(8,128)S(1)}, f32[194,128]{1,0:T(8,128)S(1)}, u32[]{:S(2)}, u32[]{:S(2)}) collective-permute-start(f32[194,128]{1,0:T(8,128)S(1)} %concatenate.13), channel_id=1, source_target_pairs={{0,6},{1,7},{2,4},{3,5},{4,2},{5,3},{6,0},{7,1},{8,14},{9,15},{10,... | collective-permute-start | bytes 297992 | tf_op jit(solution)/shard_map/ppermute | solution.py:293
  13.1 4.9 %collective-permute-start.3 = (f32[194,128]{1,0:T(8,128)S(1)}, f32[194,128]{1,0:T(8,128)S(1)}, u32[]{:S(2)}, u32[]{:S(2)}) collective-permute-start(f32[194,128]{1,0:T(8,128)S(1)} %concatenate.13), channel_id=1, source_target_pairs={{0,4},{1,5},{2,6},{3,7},{4,0},{5,1},{6,2},{7,3},{8,12},{9,13},{10,... | collective-permute-start | bytes 297992 | tf_op jit(solution)/shard_map/ppermute | solution.py:293
  13.6 4.7 %collective-permute-start.2 = (f32[194,128]{1,0:T(8,128)S(1)}, f32[194,128]{1,0:T(8,128)S(1)}, u32[]{:S(2)}, u32[]{:S(2)}) collective-permute-start(f32[194,128]{1,0:T(8,128)S(1)} %concatenate.13), channel_id=1, source_target_pairs={{0,2},{1,3},{2,0},{3,1},{4,6},{5,7},{6,4},{7,5},{8,10},{9,11},{10,... | collective-permute-start | bytes 297992 | tf_op jit(solution)/shard_map/ppermute | solution.py:293
  18.4 6.9 %collective-permute-start.5 = (f32[194,128]{1,0:T(8,128)S(1)}, f32[194,128]{1,0:T(8,128)S(1)}, u32[]{:S(2)}, u32[]{:S(2)}) collective-permute-start(f32[194,128]{1,0:T(8,128)S(1)} %concatenate.14), channel_id=1, source_target_pairs={{0,16},{1,17},{2,18},{3,19},{4,20},{5,21},{6,22},{7,23},{8,24},{9,... | collective-permute-start | bytes 297992 | tf_op jit(solution)/shard_map/ppermute | solution.py:293
  25.4 1.4 %collective-permute-start.6 = (f32[194,128]{1,0:T(8,128)S(1)}, f32[194,128]{1,0:T(8,128)S(1)}, u32[]{:S(2)}, u32[]{:S(2)}) collective-permute-start(f32[194,128]{1,0:T(8,128)S(1)} %concatenate.15.own_ref), channel_id=1, source_target_pairs={{0,1},{1,0},{2,3},{3,2},{4,5},{5,4},{6,7},{7,6},{8,9},{9,8},{10,11... | collective-permute-start | bytes 297992 | tf_op jit(solution)/shard_map/ppermute | solution.py:293
